TPU v7x, 32 devices: a whole 2x2x4 slice. The times are simulated.
32 devices in a mesh: row: 4 (over x, core), col: 8 (over z, y).
Axes of the slice: x: 2, y: 2, z: 4, core: 2. Of those that a mesh axis runs over, the one named last changes fastest.
Arguments:
- block_input: bfloat16 [2, 1152, 4096], P(None, 'col', 'row'), may hold values from -6 to 6
- text_tokens: bfloat16 [2, 480, 1152], P(None, 'row', 'col'), may hold values from -6 to 6
- text_length: int32 [2, 4], P(None, 'row'), may hold values from 1 to 120, as said below
- time_index: int32 [2, 4], P(None, 'row'), may hold values from 0 to 1023
- shift_table: float32 [6, 1152], P(None, 'col'), may hold values from -6 to 6
- time_table: float32 [6, 1152, 1024], P(None, 'col'), may hold values from -6 to 6
- query_weight: bfloat16 [1152, 1152], P('row', 'col'), may hold values from -0.1875 to 0.1875
- key_weight: bfloat16 [1152, 1152], P('row', 'col'), may hold values from -0.1875 to 0.1875
- value_weight: bfloat16 [1152, 1152], P('row', 'col'), may hold values from -0.1875 to 0.1875
- query_bias: float32 [1152], P('col'), may hold values from -4 to 4
- value_bias: float32 [1152], P('col'), may hold values from -4 to 4
- out_weight: bfloat16 [1152, 1152], P('col', 'row'), may hold values from -0.75 to 0.75
- out_bias: float32 [1152], P('col'), may hold values from -4 to 4
- cross_query: bfloat16 [1152, 1152], P('row', 'col'), may hold values from -0.1875 to 0.1875
- cross_key: bfloat16 [1152, 1152], P('row', 'col'), may hold values from -0.1875 to 0.1875
- cross_value: bfloat16 [1152, 1152], P('row', 'col'), may hold values from -0.1875 to 0.1875
- cross_query_bias: float32 [1152], P('col'), may hold values from -4 to 4
- cross_value_bias: float32 [1152], P('col'), may hold values from -4 to 4
- cross_out: bfloat16 [1152, 1152], P('col', 'row'), may hold values from -0.5 to 0.5
- cross_out_bias: float32 [1152], P('col'), may hold values from -4 to 4
- up_weight: bfloat16 [1152, 4608], P('row', 'col'), may hold values from -0.1875 to 0.1875
- up_bias: float32 [4608], P('col'), may hold values from -4 to 4
- down_weight: bfloat16 [4608, 1152], P('col', 'row'), may hold values from -0.09375 to 0.09375
- down_bias: float32 [1152], P('col'), may hold values from -4 to 4
- out_grad: bfloat16 [2, 1152, 4096], P(None, 'col', 'row'), may hold values from -6 to 6
Outputs:
- block_output: float32 [2, 1152, 4096], P(None, 'col', 'row')
- grad_input: float32 [2, 1152, 4096], P(None, 'col', 'row')
- grad_text: float32 [2, 480, 1152], P(None, 'row', 'col')
- grad_shift_table: float32 [6, 1152], P(None, 'col')
- grad_time_table: float32 [6, 1152, 1024], P(None, 'col')
- grad_query_weight: float32 [1152, 1152], P('row', 'col')
- grad_key_weight: float32 [1152, 1152], P('row', 'col')
- grad_value_weight: float32 [1152, 1152], P('row', 'col')
- grad_query_bias: float32 [1152], P('col')
- grad_value_bias: float32 [1152], P('col')
- grad_out_weight: float32 [1152, 1152], P('col', 'row')
- grad_out_bias: float32 [1152], P('col')
- grad_cross_query: float32 [1152, 1152], P('row', 'col')
- grad_cross_key: float32 [1152, 1152], P('row', 'col')
- grad_cross_value: float32 [1152, 1152], P('row', 'col')
- grad_cross_query_bias: float32 [1152], P('col')
- grad_cross_value_bias: float32 [1152], P('col')
- grad_cross_out: float32 [1152, 1152], P('col', 'row')
- grad_cross_out_bias: float32 [1152], P('col')
- grad_up_weight: float32 [1152, 4608], P('row', 'col')
- grad_up_bias: float32 [4608], P('col')
- grad_down_weight: float32 [4608, 1152], P('col', 'row')
- grad_down_bias: float32 [1152], P('col')
Inputs may be any that keep to these rules, and one draw needn't show every extreme that they name: Caption keys at positions text_length and beyond are masked; in each micro-batch one latent has all 120 text tokens and another has one.
All inputs are finite; a program needn't handle non-finite values.
Results may differ from a plain program's by a relative error of at most 0.02.
Values may be sent and summed in bfloat16 or wider, within the bound.
A program may use at most 192 MiB of HBM per device.

v0:
```python
import jax
import jax.numpy as jnp
from jax import lax
from jax.sharding import PartitionSpec as P

D = 1152
HEADS = 16
HD = 72


NORM_EPS = 1e-06
MASK_FILL = -1e30


def matmul_f(first_op, second_op):
    return jnp.dot(first_op, second_op, preferred_element_type=jnp.float32)


def matmul_tn(first_op, second_op):
    return lax.dot_general(
        first_op, second_op, (((0,), (0,)), ((), ())), preferred_element_type=jnp.float32
    )


def matmul_nt(first_op, second_op):
    return lax.dot_general(
        first_op, second_op, (((1,), (1,)), ((), ())), preferred_element_type=jnp.float32
    )


def gelu_tanh(pre_act):
    return jax.nn.gelu(pre_act, approximate=True)


def token_sums(first_in, second_in):
    return lax.psum((jnp.sum(first_in, axis=-1), jnp.sum(second_in, axis=-1)), "col")


def gather_cols(modulated):
    return lax.all_gather(modulated, "col", axis=1, tiled=True)


def reduce_cols(partial_sum):
    return lax.psum_scatter(partial_sum, "col", scatter_dimension=1, tiled=True)


def gather_grads(gradient):
    return lax.all_gather(gradient, "col", axis=1, tiled=True)


def reduce_grads(partial_sum):
    return lax.psum_scatter(partial_sum, "col", scatter_dimension=1, tiled=True)


def norm_forward(resid, shift_vec, scale_vec, features):
    sum_total, square = token_sums(resid, resid * resid)
    average = sum_total / features
    variance = square / features - average * average
    inv_std = lax.rsqrt(variance + NORM_EPS)
    normed = (resid - average[..., None]) * inv_std[..., None]
    modulated = normed * (1.0 + scale_vec[:, None, :]) + shift_vec[:, None, :]
    return (normed, inv_std, modulated.astype(jnp.bfloat16))


def norm_backward(gradient, normed, inv_std, scale_vec, features):
    grad_norm = gradient * (1.0 + scale_vec[:, None, :])
    first_sum, second_sum = token_sums(grad_norm, grad_norm * normed)
    backward = inv_std[..., None] * (
        grad_norm - first_sum[..., None] / features - normed * (second_sum[..., None] / features)
    )
    return (backward, jnp.sum(gradient, axis=1), jnp.sum(gradient * normed, axis=1))


def score_block(queries, key_rows, key_valid, score_scale):
    scores = (
        jnp.einsum("qhd,khd->hqk", queries, key_rows, preferred_element_type=jnp.float32)
        * score_scale
    )
    if key_valid is not None:
        scores = jnp.where(key_valid[None, None, :], scores, MASK_FILL)
    return scores


def attend_forward(queries, key_rows, values_in, key_valid, score_scale):
    scores = score_block(queries, key_rows, key_valid, score_scale)
    row_top = jnp.max(scores, axis=-1, keepdims=True)
    log_total = row_top + jnp.log(jnp.sum(jnp.exp(scores - row_top), axis=-1, keepdims=True))
    attn_probs = jnp.exp(scores - log_total).astype(jnp.bfloat16)
    attn_out = jnp.einsum("hqk,khd->qhd", attn_probs, values_in, preferred_element_type=jnp.float32)
    return (attn_out.reshape(attn_out.shape[0], -1).astype(jnp.bfloat16), log_total)


def attend_backward(queries, key_rows, values_in, key_valid, log_total, grad_out, score_scale):
    scores = score_block(queries, key_rows, key_valid, score_scale)
    attn_probs = jnp.exp(scores - log_total)
    grad_values = jnp.einsum(
        "hqk,qhd->khd",
        attn_probs.astype(jnp.bfloat16),
        grad_out,
        preferred_element_type=jnp.float32,
    )
    grad_probs = jnp.einsum("qhd,khd->hqk", grad_out, values_in, preferred_element_type=jnp.float32)
    grad_scores = attn_probs * (
        grad_probs - jnp.sum(grad_probs * attn_probs, axis=-1, keepdims=True)
    )
    grad_scores = (grad_scores * score_scale).astype(jnp.bfloat16)
    grad_queries = jnp.einsum(
        "hqk,khd->qhd", grad_scores, key_rows, preferred_element_type=jnp.float32
    )
    grad_keys = jnp.einsum("hqk,qhd->khd", grad_scores, queries, preferred_element_type=jnp.float32)
    return (
        grad_queries.astype(jnp.bfloat16),
        grad_keys.astype(jnp.bfloat16),
        grad_values.astype(jnp.bfloat16),
    )


def shards(
    block_input,
    text_tokens,
    text_length,
    time_index,
    shift_table,
    time_table,
    query_weight,
    key_weight,
    value_weight,
    query_bias,
    value_bias,
    out_weight,
    out_bias,
    cross_query,
    cross_key,
    cross_value,
    cross_query_bias,
    cross_value_bias,
    cross_out,
    cross_out_bias,
    up_weight,
    up_bias,
    down_weight,
    down_bias,
    out_grad,
):
    col_count = lax.axis_size("col")
    feat_cols = block_input.shape[1]
    latents = text_length.shape[1]
    tok_rows = block_input.shape[2]
    length = tok_rows // latents
    text_rows = text_tokens.shape[1] // latents
    local_heads = HEADS // col_count
    score_scale = HD ** (-0.5)
    steps_count = time_table.shape[2]
    features = float(D)
    (
        query_full,
        key_full,
        value_full,
        cquery_full,
        ckey_full,
        cvalue_full,
        up_full,
        out_full,
        cout_full,
        down_full,
    ) = (
        lax.all_gather(query_weight, "row", axis=0, tiled=True),
        lax.all_gather(key_weight, "row", axis=0, tiled=True),
        lax.all_gather(value_weight, "row", axis=0, tiled=True),
        lax.all_gather(cross_query, "row", axis=0, tiled=True),
        lax.all_gather(cross_key, "row", axis=0, tiled=True),
        lax.all_gather(cross_value, "row", axis=0, tiled=True),
        lax.all_gather(up_weight, "row", axis=0, tiled=True),
        lax.all_gather(out_weight, "row", axis=1, tiled=True),
        lax.all_gather(cross_out, "row", axis=1, tiled=True),
        lax.all_gather(down_weight, "row", axis=1, tiled=True),
    )
    out_used, cout_used = (out_full, cout_full)
    time_flat = time_table.reshape(6 * feat_cols, steps_count)
    step_ids = jnp.arange(steps_count, dtype=jnp.int32)

    def heads_view(matrix, count):
        return matrix.reshape(latents, count, local_heads, HD)

    def self_forward(pack):
        return attend_forward(pack[0], pack[1], pack[2], None, score_scale)

    def cross_forward(pack):
        return attend_forward(pack[0], pack[1], pack[2], pack[3], score_scale)

    def self_backward(pack):
        return attend_backward(pack[0], pack[1], pack[2], None, pack[3], pack[4], score_scale)

    def cross_backward(pack):
        return attend_backward(pack[0], pack[1], pack[2], pack[3], pack[4], pack[5], score_scale)

    def micro_step(totals, inputs_m):
        x_block, text_block, lengths_m, index_m, grad_block = inputs_m
        onehot = (index_m[:, None] == step_ids[None, :]).astype(jnp.float32)
        modulation = lax.dot_general(
            onehot,
            time_flat,
            (((1,), (1,)), ((), ())),
            precision=lax.Precision.HIGHEST,
            preferred_element_type=jnp.float32,
        )
        modulation = modulation.reshape(latents, 6, feat_cols) + shift_table[None]
        gate_attn = modulation[:, 2][:, None, :]
        gate_mlp = modulation[:, 5][:, None, :]
        resid = x_block.astype(jnp.float32).T.reshape(latents, length, feat_cols)
        normed_a, inv_a, attn_in = norm_forward(resid, modulation[:, 0], modulation[:, 1], features)
        attn_full = gather_cols(attn_in.reshape(tok_rows, feat_cols))
        queries = (matmul_f(attn_full, query_full) + query_bias).astype(jnp.bfloat16)
        key_rows = matmul_f(attn_full, key_full).astype(jnp.bfloat16)
        values_s = (matmul_f(attn_full, value_full) + value_bias).astype(jnp.bfloat16)
        self_pack = (
            heads_view(queries, length),
            heads_view(key_rows, length),
            heads_view(values_s, length),
        )
        attn_out, attn_lse = lax.map(self_forward, self_pack)
        attn_out = attn_out.reshape(tok_rows, feat_cols)
        attn_proj = reduce_cols(matmul_f(attn_out, out_used))
        attn_branch = (attn_proj + out_bias).reshape(latents, length, feat_cols)
        after_attn = resid + gate_attn * attn_branch
        cross_in = after_attn.reshape(tok_rows, feat_cols).astype(jnp.bfloat16)
        cross_full, text_full = (
            lax.all_gather(cross_in, "col", axis=1, tiled=True),
            lax.all_gather(text_block, "col", axis=1, tiled=True),
        )
        cross_q = (matmul_f(cross_full, cquery_full) + cross_query_bias).astype(jnp.bfloat16)
        cross_k = matmul_f(text_full, ckey_full).astype(jnp.bfloat16)
        cross_v = (matmul_f(text_full, cvalue_full) + cross_value_bias).astype(jnp.bfloat16)
        key_valid = jnp.arange(text_rows, dtype=jnp.int32)[None, :] < lengths_m[:, None]
        cross_pack = (
            heads_view(cross_q, length),
            heads_view(cross_k, text_rows),
            heads_view(cross_v, text_rows),
            key_valid,
        )
        cross_att, cross_lse = lax.map(cross_forward, cross_pack)
        cross_att = cross_att.reshape(tok_rows, feat_cols)
        cross_proj = reduce_cols(matmul_f(cross_att, cout_used))
        cross_branch = cross_proj + cross_out_bias
        after_cross = after_attn + cross_branch.reshape(latents, length, feat_cols)
        normed_m, inv_m, mlp_in = norm_forward(
            after_cross, modulation[:, 3], modulation[:, 4], features
        )
        mlp_full = gather_cols(mlp_in.reshape(tok_rows, feat_cols))
        hidden_pre = matmul_f(mlp_full, up_full) + up_bias
        hidden_val, gelu_pull = jax.vjp(gelu_tanh, hidden_pre)
        hidden_act = hidden_val.astype(jnp.bfloat16)
        mlp_sum = reduce_cols(matmul_f(hidden_act, down_full))
        mlp_branch = (mlp_sum + down_bias).reshape(latents, length, feat_cols)
        result = after_cross + gate_mlp * mlp_branch
        grad_res = grad_block.astype(jnp.float32).T.reshape(latents, length, feat_cols)
        grad_gate_m = jnp.sum(grad_res * mlp_branch, axis=1)
        grad_mlp = (gate_mlp * grad_res).reshape(tok_rows, feat_cols)
        grad_mrows = gather_grads(grad_mlp.astype(jnp.bfloat16))
        grad_act = matmul_nt(grad_mrows, down_full)
        grad_pre = gelu_pull(grad_act)[0].astype(jnp.bfloat16)
        grad_mlp_in = reduce_grads(matmul_nt(grad_pre, up_full))
        back_m, shift_m_grad, scale_m_grad = norm_backward(
            grad_mlp_in.reshape(latents, length, feat_cols),
            normed_m,
            inv_m,
            modulation[:, 4],
            features,
        )
        grad_cross = grad_res + back_m
        grad_cross_rows = grad_cross.reshape(tok_rows, feat_cols)
        grad_cross_low = grad_cross_rows.astype(jnp.bfloat16)
        grad_cfull = gather_grads(grad_cross_low)
        grad_catt = matmul_nt(grad_cfull, cout_used).astype(jnp.bfloat16)
        dquery_c, dkey_c, dvalue_c = lax.map(
            cross_backward, cross_pack + (cross_lse, heads_view(grad_catt, length))
        )
        dquery_c = dquery_c.reshape(tok_rows, feat_cols)
        dkey_c = dkey_c.reshape(latents * text_rows, feat_cols)
        dvalue_c = dvalue_c.reshape(latents * text_rows, feat_cols)
        grad_cin, grad_text = (
            lax.psum_scatter(
                matmul_nt(dquery_c, cquery_full), "col", scatter_dimension=1, tiled=True
            ),
            lax.psum_scatter(
                matmul_nt(dkey_c, ckey_full) + matmul_nt(dvalue_c, cvalue_full),
                "col",
                scatter_dimension=1,
                tiled=True,
            ),
        )
        grad_attn_res = grad_cross + grad_cin.reshape(latents, length, feat_cols)
        grad_gate_a = jnp.sum(grad_attn_res * attn_branch, axis=1)
        grad_attn = (gate_attn * grad_attn_res).reshape(tok_rows, feat_cols)
        grad_attn_low = grad_attn.astype(jnp.bfloat16)
        grad_afull = gather_grads(grad_attn_low)
        grad_aatt = matmul_nt(grad_afull, out_used).astype(jnp.bfloat16)
        dquery_s, dkey_s, dvalue_s = lax.map(
            self_backward, self_pack + (attn_lse, heads_view(grad_aatt, length))
        )
        dquery_s = dquery_s.reshape(tok_rows, feat_cols)
        dkey_s = dkey_s.reshape(tok_rows, feat_cols)
        dvalue_s = dvalue_s.reshape(tok_rows, feat_cols)
        grad_ain = reduce_grads(
            matmul_nt(dquery_s, query_full)
            + matmul_nt(dkey_s, key_full)
            + matmul_nt(dvalue_s, value_full)
        )
        back_a, shift_a_grad, scale_a_grad = norm_backward(
            grad_ain.reshape(latents, length, feat_cols),
            normed_a,
            inv_a,
            modulation[:, 1],
            features,
        )
        grad_input = grad_attn_res + back_a
        grad_mod = jnp.stack(
            [shift_a_grad, scale_a_grad, grad_gate_a, shift_m_grad, scale_m_grad, grad_gate_m],
            axis=1,
        )
        time_update = lax.dot_general(
            grad_mod.reshape(latents, 6 * feat_cols),
            onehot,
            (((0,), (0,)), ((), ())),
            precision=lax.Precision.HIGHEST,
            preferred_element_type=jnp.float32,
        )
        updates = (
            matmul_tn(attn_full, dquery_s),
            matmul_tn(attn_full, dkey_s),
            matmul_tn(attn_full, dvalue_s),
            matmul_tn(cross_full, dquery_c),
            matmul_tn(text_full, dkey_c),
            matmul_tn(text_full, dvalue_c),
            matmul_tn(mlp_full, grad_pre),
            matmul_tn(attn_out, grad_afull),
            matmul_tn(cross_att, grad_cfull),
            matmul_tn(hidden_act, grad_mrows),
            jnp.sum(dquery_s.astype(jnp.float32), axis=0),
            jnp.sum(dvalue_s.astype(jnp.float32), axis=0),
            jnp.sum(grad_attn, axis=0),
            jnp.sum(dquery_c.astype(jnp.float32), axis=0),
            jnp.sum(dvalue_c.astype(jnp.float32), axis=0),
            jnp.sum(grad_cross_rows, axis=0),
            jnp.sum(grad_pre.astype(jnp.float32), axis=0),
            jnp.sum(grad_mlp, axis=0),
            jnp.sum(grad_mod, axis=0),
            time_update,
        )
        totals = tuple((earlier_sum + added_sum for earlier_sum, added_sum in zip(totals, updates)))
        return (
            totals,
            (
                result.reshape(tok_rows, feat_cols).T,
                grad_input.reshape(tok_rows, feat_cols).T,
                grad_text,
            ),
        )

    templates = (
        query_full,
        key_full,
        value_full,
        cquery_full,
        ckey_full,
        cvalue_full,
        up_full,
        out_used,
        cout_used,
        down_full,
        query_bias,
        value_bias,
        out_bias,
        cross_query_bias,
        cross_value_bias,
        cross_out_bias,
        up_bias,
        down_bias,
        shift_table,
        time_flat,
    )
    start_sums = tuple((jnp.zeros(template.shape, jnp.float32) for template in templates))
    totals, (block_output, grad_inputs, grad_texts) = lax.scan(
        micro_step, start_sums, (block_input, text_tokens, text_length, time_index, out_grad)
    )
    (
        sum_query,
        sum_key,
        sum_value,
        sum_cquery,
        sum_ckey,
        sum_cvalue,
        sum_up,
        sum_out,
        sum_cout,
        sum_down,
        sum_qbias,
        sum_vbias,
        sum_obias,
        sum_cqbias,
        sum_cvbias,
        sum_cobias,
        sum_upbias,
        sum_downbias,
        sum_shift,
        sum_time,
    ) = totals
    (
        sum_query,
        sum_key,
        sum_value,
        sum_cquery,
        sum_ckey,
        sum_cvalue,
        sum_up,
        sum_out,
        sum_cout,
        sum_down,
    ) = (
        lax.psum_scatter(sum_query, "row", scatter_dimension=0, tiled=True),
        lax.psum_scatter(sum_key, "row", scatter_dimension=0, tiled=True),
        lax.psum_scatter(sum_value, "row", scatter_dimension=0, tiled=True),
        lax.psum_scatter(sum_cquery, "row", scatter_dimension=0, tiled=True),
        lax.psum_scatter(sum_ckey, "row", scatter_dimension=0, tiled=True),
        lax.psum_scatter(sum_cvalue, "row", scatter_dimension=0, tiled=True),
        lax.psum_scatter(sum_up, "row", scatter_dimension=0, tiled=True),
        lax.psum_scatter(sum_out, "row", scatter_dimension=1, tiled=True),
        lax.psum_scatter(sum_cout, "row", scatter_dimension=1, tiled=True),
        lax.psum_scatter(sum_down, "row", scatter_dimension=1, tiled=True),
    )
    (
        sum_qbias,
        sum_vbias,
        sum_obias,
        sum_cqbias,
        sum_cvbias,
        sum_cobias,
        sum_upbias,
        sum_downbias,
        sum_shift,
        sum_time,
    ) = lax.psum(
        (
            sum_qbias,
            sum_vbias,
            sum_obias,
            sum_cqbias,
            sum_cvbias,
            sum_cobias,
            sum_upbias,
            sum_downbias,
            sum_shift,
            sum_time,
        ),
        "row",
    )
    return (
        block_output,
        grad_inputs,
        grad_texts,
        sum_shift,
        sum_time.reshape(6, feat_cols, steps_count),
        sum_query,
        sum_key,
        sum_value,
        sum_qbias,
        sum_vbias,
        sum_out,
        sum_obias,
        sum_cquery,
        sum_ckey,
        sum_cvalue,
        sum_cqbias,
        sum_cvbias,
        sum_cout,
        sum_cobias,
        sum_up,
        sum_upbias,
        sum_down,
        sum_downbias,
    )


def solution(mesh):
    return jax.shard_map(
        shards,
        mesh=mesh,
        in_specs=(
            P(None, "col", "row"),
            P(None, "row", "col"),
            P(None, "row"),
            P(None, "row"),
            P(None, "col"),
            P(None, "col", None),
            P("row", "col"),
            P("row", "col"),
            P("row", "col"),
            P("col"),
            P("col"),
            P("col", "row"),
            P("col"),
            P("row", "col"),
            P("row", "col"),
            P("row", "col"),
            P("col"),
            P("col"),
            P("col", "row"),
            P("col"),
            P("row", "col"),
            P("col"),
            P("col", "row"),
            P("col"),
            P(None, "col", "row"),
        ),
        out_specs=(
            P(None, "col", "row"),
            P(None, "col", "row"),
            P(None, "row", "col"),
            P(None, "col"),
            P(None, "col", None),
            P("row", "col"),
            P("row", "col"),
            P("row", "col"),
            P("col"),
            P("col"),
            P("col", "row"),
            P("col"),
            P("row", "col"),
            P("row", "col"),
            P("row", "col"),
            P("col"),
            P("col"),
            P("col", "row"),
            P("col"),
            P("row", "col"),
            P("col"),
            P("col", "row"),
            P("col"),
        ),
        check_vma=False,
    )
```

profile of v0, /device:TPU:0, one launch (start us, length us, event | category | flops | bytes accessed | tf_op | source)
XLA Modules:
  0.0 2694.1 jit_solution(3759740545114773296)
XLA Ops:
  81.6 2220.4 %while.53 = (s32[]{:T(128)}, f32[1152,144]{0,1:T(8,128)}, f32[1152,144]{0,1:T(8,128)}, f32[1152,144]{0,1:T(8,128)}, f32[1152,144]{0,1:T(8,128)}, /*index=5*/f32[...) while((s32[]{:T(128)}, f32[1152,144]{0,1:T(8,128)}, ...), condition=%wide.region_44.45_spmd.clone, body=%wide.region_0.44_spmd.clone.sunk | while | flops 16661160960 | bytes 606032064 | solution.py:383
  111.4 48.9 %all-gather.25.cloned.1.call-done = bf16[1024,1152]{0,1:T(8,128)(2,1)} async-done(((bf16[1024,144]{0,1:T(8,128)(2,1)}), bf16[1024,1152]{0,1:T(8,128)(2,1)}) %all-gather.25.cloned.1.call-update) | async-done | bytes 2359312 | tf_op jit(solution)/shard_map/while/body/eval_jaxpr/all_gather | solution.py:40
  174.7 94.3 %reduce-scatter.54.cloned.1.call-done = f32[1024,144]{0,1:T(8,128)} async-done(((f32[1024,1152]{0,1:T(8,128)}), f32[1024,144]{0,1:T(8,128)}) %reduce-scatter.54.cloned.1.call-update) | async-done | bytes 589840 | tf_op jit(solution)/shard_map/while/body/eval_jaxpr/reduce_scatter | solution.py:44
  274.3 31.8 %all-gather.11 = bf16[1,120,1152]{1,2,0:T(8,128)(2,1)S(1)} all-gather(bf16[1,120,144]{1,2,0:T(8,128)(2,1)S(1)} %constant_dynamic-slice_fusion.7), channel_id=2, replica_groups=mesh['row'=4,'col'=8] {'col'}, dimensions={2}, use_global_device_ids=true | all-gather | bytes 311040 | tf_op jit(solution)/shard_map/while/body/eval_jaxpr/all_gather | solution.py:229
  330.9 94.5 %reduce-scatter.56.cloned.1.call-done = f32[1024,144]{0,1:T(8,128)} async-done(((f32[1024,1152]{0,1:T(8,128)}), f32[1024,144]{0,1:T(8,128)}) %reduce-scatter.56.cloned.1.call-update) | async-done | bytes 589840 | tf_op jit(solution)/shard_map/while/body/eval_jaxpr/reduce_scatter | solution.py:44
  450.7 49.2 %all-gather.29.cloned.1.call-done = bf16[1024,1152]{0,1:T(8,128)(2,1)} async-done(((bf16[1024,144]{0,1:T(8,128)(2,1)}), bf16[1024,1152]{0,1:T(8,128)(2,1)}) %all-gather.29.cloned.1.call-update) | async-done | bytes 2359312 | tf_op jit(solution)/shard_map/while/body/eval_jaxpr/all_gather | solution.py:40
  510.1 94.3 %reduce-scatter.58.cloned.1.call-done = f32[1024,144]{0,1:T(8,128)} async-done(((f32[1024,1152]{0,1:T(8,128)}), f32[1024,144]{0,1:T(8,128)}) %reduce-scatter.58.cloned.1.call-update) | async-done | bytes 589840 | tf_op jit(solution)/shard_map/while/body/eval_jaxpr/reduce_scatter | solution.py:44
  607.1 51.6 %all-gather.31.cloned.1.call-done = bf16[1024,1152]{0,1:T(8,128)(2,1)} async-done(((bf16[1024,144]{0,1:T(8,128)(2,1)}), bf16[1024,1152]{0,1:T(8,128)(2,1)}) %all-gather.31.cloned.1.call-update) | async-done | bytes 2359312 | tf_op jit(solution)/shard_map/while/body/eval_jaxpr/all_gather | solution.py:48
  670.5 94.3 %reduce-scatter.60.cloned.1.call-done = f32[1024,144]{0,1:T(8,128)} async-done(((f32[1024,1152]{0,1:T(8,128)}), f32[1024,144]{0,1:T(8,128)}) %reduce-scatter.60.cloned.1.call-update) | async-done | bytes 589840 | tf_op jit(solution)/shard_map/while/body/eval_jaxpr/reduce_scatter | solution.py:52
  791.0 49.2 %all-gather.33.cloned.1.call-done = bf16[1024,1152]{0,1:T(8,128)(2,1)} async-done(((bf16[1024,144]{0,1:T(8,128)(2,1)}), bf16[1024,1152]{0,1:T(8,128)(2,1)}) %all-gather.33.cloned.1.call-update) | async-done | bytes 2359312 | tf_op jit(solution)/shard_map/while/body/eval_jaxpr/all_gather | solution.py:48
  852.1 94.3 %reduce-scatter.62.cloned.1.call-done = f32[1024,144]{0,1:T(8,128)} async-done(((f32[1024,1152]{0,1:T(8,128)}), f32[1024,144]{0,1:T(8,128)}) %reduce-scatter.62.cloned.1.call-update) | async-done | bytes 589840 | tf_op jit(solution)/shard_map/while/body/eval_jaxpr/reduce_scatter | solution.py:282
  957.9 44.1 %all-gather.35.cloned.1.call-done = bf16[1024,1152]{0,1:T(8,128)(2,1)} async-done(((bf16[1024,144]{0,1:T(8,128)(2,1)}), bf16[1024,1152]{0,1:T(8,128)(2,1)}) %all-gather.35.cloned.1.call-update) | async-done | bytes 2359312 | tf_op jit(solution)/shard_map/while/body/eval_jaxpr/all_gather | solution.py:48
  1081.5 83.1 %reduce-scatter.64.cloned.1.call-done = f32[1024,144]{0,1:T(8,128)} async-done(((f32[1024,1152]{0,1:T(8,128)}), f32[1024,144]{0,1:T(8,128)}) %reduce-scatter.64.cloned.1.call-update) | async-done | bytes 589840 | tf_op jit(solution)/shard_map/while/body/eval_jaxpr/reduce_scatter | solution.py:52
  1215.4 50.5 %all-gather.25.cloned.1.call-done = bf16[1024,1152]{0,1:T(8,128)(2,1)} async-done(((bf16[1024,144]{0,1:T(8,128)(2,1)}), bf16[1024,1152]{0,1:T(8,128)(2,1)}) %all-gather.25.cloned.1.call-update) | async-done | bytes 2359312 | tf_op jit(solution)/shard_map/while/body/eval_jaxpr/all_gather | solution.py:40
  1280.4 94.3 %reduce-scatter.54.cloned.1.call-done = f32[1024,144]{0,1:T(8,128)} async-done(((f32[1024,1152]{0,1:T(8,128)}), f32[1024,144]{0,1:T(8,128)}) %reduce-scatter.54.cloned.1.call-update) | async-done | bytes 589840 | tf_op jit(solution)/shard_map/while/body/eval_jaxpr/reduce_scatter | solution.py:44
  1379.9 31.8 %all-gather.11 = bf16[1,120,1152]{1,2,0:T(8,128)(2,1)S(1)} all-gather(bf16[1,120,144]{1,2,0:T(8,128)(2,1)S(1)} %constant_dynamic-slice_fusion.7), channel_id=2, replica_groups=mesh['row'=4,'col'=8] {'col'}, dimensions={2}, use_global_device_ids=true | all-gather | bytes 311040 | tf_op jit(solution)/shard_map/while/body/eval_jaxpr/all_gather | solution.py:229
  1436.6 94.4 %reduce-scatter.56.cloned.1.call-done = f32[1024,144]{0,1:T(8,128)} async-done(((f32[1024,1152]{0,1:T(8,128)}), f32[1024,144]{0,1:T(8,128)}) %reduce-scatter.56.cloned.1.call-update) | async-done | bytes 589840 | tf_op jit(solution)/shard_map/while/body/eval_jaxpr/reduce_scatter | solution.py:44
  1556.0 49.2 %all-gather.29.cloned.1.call-done = bf16[1024,1152]{0,1:T(8,128)(2,1)} async-done(((bf16[1024,144]{0,1:T(8,128)(2,1)}), bf16[1024,1152]{0,1:T(8,128)(2,1)}) %all-gather.29.cloned.1.call-update) | async-done | bytes 2359312 | tf_op jit(solution)/shard_map/while/body/eval_jaxpr/all_gather | solution.py:40
  1615.3 94.3 %reduce-scatter.58.cloned.1.call-done = f32[1024,144]{0,1:T(8,128)} async-done(((f32[1024,1152]{0,1:T(8,128)}), f32[1024,144]{0,1:T(8,128)}) %reduce-scatter.58.cloned.1.call-update) | async-done | bytes 589840 | tf_op jit(solution)/shard_map/while/body/eval_jaxpr/reduce_scatter | solution.py:44
  1712.4 51.6 %all-gather.31.cloned.1.call-done = bf16[1024,1152]{0,1:T(8,128)(2,1)} async-done(((bf16[1024,144]{0,1:T(8,128)(2,1)}), bf16[1024,1152]{0,1:T(8,128)(2,1)}) %all-gather.31.cloned.1.call-update) | async-done | bytes 2359312 | tf_op jit(solution)/shard_map/while/body/eval_jaxpr/all_gather | solution.py:48
  1775.7 94.3 %reduce-scatter.60.cloned.1.call-done = f32[1024,144]{0,1:T(8,128)} async-done(((f32[1024,1152]{0,1:T(8,128)}), f32[1024,144]{0,1:T(8,128)}) %reduce-scatter.60.cloned.1.call-update) | async-done | bytes 589840 | tf_op jit(solution)/shard_map/while/body/eval_jaxpr/reduce_scatter | solution.py:52
  1896.3 49.1 %all-gather.33.cloned.1.call-done = bf16[1024,1152]{0,1:T(8,128)(2,1)} async-done(((bf16[1024,144]{0,1:T(8,128)(2,1)}), bf16[1024,1152]{0,1:T(8,128)(2,1)}) %all-gather.33.cloned.1.call-update) | async-done | bytes 2359312 | tf_op jit(solution)/shard_map/while/body/eval_jaxpr/all_gather | solution.py:48
  1957.3 94.3 %reduce-scatter.62.cloned.1.call-done = f32[1024,144]{0,1:T(8,128)} async-done(((f32[1024,1152]{0,1:T(8,128)}), f32[1024,144]{0,1:T(8,128)}) %reduce-scatter.62.cloned.1.call-update) | async-done | bytes 589840 | tf_op jit(solution)/shard_map/while/body/eval_jaxpr/reduce_scatter | solution.py:282
  2063.1 44.0 %all-gather.35.cloned.1.call-done = bf16[1024,1152]{0,1:T(8,128)(2,1)} async-done(((bf16[1024,144]{0,1:T(8,128)(2,1)}), bf16[1024,1152]{0,1:T(8,128)(2,1)}) %all-gather.35.cloned.1.call-update) | async-done | bytes 2359312 | tf_op jit(solution)/shard_map/while/body/eval_jaxpr/all_gather | solution.py:48
  2192.8 77.2 %reduce-scatter.64.cloned.1.call-done = f32[1024,144]{0,1:T(8,128)} async-done(((f32[1024,1152]{0,1:T(8,128)}), f32[1024,144]{0,1:T(8,128)}) %reduce-scatter.64.cloned.1.call-update) | async-done | bytes 589840 | tf_op jit(solution)/shard_map/while/body/eval_jaxpr/reduce_scatter | solution.py:52
  2358.3 26.4 reduce-scatter.38.cloned.1.call-done
  2386.5 26.4 reduce-scatter.40.cloned.1.call-done
  2442.8 26.4 reduce-scatter.46.cloned.1.call-done
  2471.0 26.4 reduce-scatter.48.cloned.1.call-done
  2527.3 75.9 %all-reduce.15.cloned.1.call-done = f32[6,144,1024]{2,1,0:T(8,128)} async-done(((f32[6,144,1024]{2,1,0:T(8,128)}), f32[6,144,1024]{2,1,0:T(8,128)}) %all-reduce.15.cloned.1.call-update) | async-done | bytes 3538960 | tf_op jit(solution)/shard_map/psum | solution.py:442
  2603.2 39.9 %reduce-scatter.34.cloned.1.call-done = f32[288,576]{1,0:T(8,128)} async-done(((f32[1152,576]{1,0:T(8,128)}), f32[288,576]{1,0:T(8,128)}) %reduce-scatter.34.cloned.1.call-update) | async-done | bytes 663568 | tf_op jit(solution)/shard_map/reduce_scatter | solution.py:426
  2643.1 39.6 %reduce-scatter.36.cloned.1.call-done = f32[576,288]{0,1:T(8,128)} async-done(((f32[576,1152]{0,1:T(8,128)}), f32[576,288]{0,1:T(8,128)}) %reduce-scatter.36.cloned.1.call-update) | async-done | bytes 663568 | tf_op jit(solution)/shard_map/reduce_scatter | solution.py:429
  (754 shorter events, 756.3 us)
Async XLA Ops:
  111.4 157.7 %reduce-scatter.54.cloned.1.call-start = ((), (), s32[]{:S(2)}) async-start(), calls=%async_computation.31 | async-start | bytes 5308416 | tf_op jit(solution)/shard_map/while/body/eval_jaxpr/reduce_scatter | solution.py:44
  174.7 148.9 %all-gather.27.cloned.1.call-start = ((), (), s32[]{:S(2)}) async-start(), calls=%async_computation.32 | async-start | bytes 2654208 | tf_op jit(solution)/shard_map/while/body/eval_jaxpr/all_gather | solution.py:228
  271.0 154.3 %reduce-scatter.56.cloned.1.call-start = ((), (), s32[]{:S(2)}) async-start(), calls=%async_computation.33 | async-start | bytes 5308416 | tf_op jit(solution)/shard_map/while/body/eval_jaxpr/reduce_scatter | solution.py:44
  330.8 169.0 %all-gather.29.cloned.1.call-start = ((), (), s32[]{:S(2)}) async-start(), calls=%async_computation.34 | async-start | bytes 2654208 | tf_op jit(solution)/shard_map/while/body/eval_jaxpr/all_gather | solution.py:40
  450.7 153.7 %reduce-scatter.58.cloned.1.call-start = ((), (), s32[]{:S(2)}) async-start(), calls=%async_computation.35 | async-start | bytes 5308416 | tf_op jit(solution)/shard_map/while/body/eval_jaxpr/reduce_scatter | solution.py:44
  510.0 148.6 %all-gather.31.cloned.1.call-start = ((), (), s32[]{:S(2)}) async-start(), calls=%async_computation.36 | async-start | bytes 2654208 | tf_op jit(solution)/shard_map/while/body/eval_jaxpr/all_gather | solution.py:48
  607.0 157.7 %reduce-scatter.60.cloned.1.call-start = ((), (), s32[]{:S(2)}) async-start(), calls=%async_computation.37 | async-start | bytes 5308416 | tf_op jit(solution)/shard_map/while/body/eval_jaxpr/reduce_scatter | solution.py:52
  670.4 169.8 %all-gather.33.cloned.1.call-start = ((), (), s32[]{:S(2)}) async-start(), calls=%async_computation.38 | async-start | bytes 2654208 | tf_op jit(solution)/shard_map/while/body/eval_jaxpr/all_gather | solution.py:48
  791.0 155.4 %reduce-scatter.62.cloned.1.call-start = ((), (), s32[]{:S(2)}) async-start(), calls=%async_computation.39 | async-start | bytes 5308416 | tf_op jit(solution)/shard_map/while/body/eval_jaxpr/reduce_scatter | solution.py:282
  852.0 149.9 %all-gather.35.cloned.1.call-start = ((), (), s32[]{:S(2)}) async-start(), calls=%async_computation.40 | async-start | bytes 2654208 | tf_op jit(solution)/shard_map/while/body/eval_jaxpr/all_gather | solution.py:48
  950.3 121.7 %reduce-scatter.66.cloned.1.call-start = ((), (), s32[]{:S(2)}) async-start(), calls=%async_computation.42 | async-start | bytes 663552 | tf_op jit(solution)/shard_map/while/body/eval_jaxpr/reduce_scatter | solution.py:285
  957.8 206.8 %reduce-scatter.64.cloned.1.call-start = ((), (), s32[]{:S(2)}) async-start(), calls=%async_computation.41 | async-start | bytes 5308416 | tf_op jit(solution)/shard_map/while/body/eval_jaxpr/reduce_scatter | solution.py:52
  1215.4 159.3 %reduce-scatter.54.cloned.1.call-start = ((), (), s32[]{:S(2)}) async-start(), calls=%async_computation.31 | async-start | bytes 5308416 | tf_op jit(solution)/shard_map/while/body/eval_jaxpr/reduce_scatter | solution.py:44
  1280.4 148.9 %all-gather.27.cloned.1.call-start = ((), (), s32[]{:S(2)}) async-start(), calls=%async_computation.32 | async-start | bytes 2654208 | tf_op jit(solution)/shard_map/while/body/eval_jaxpr/all_gather | solution.py:228
  1376.7 154.3 %reduce-scatter.56.cloned.1.call-start = ((), (), s32[]{:S(2)}) async-start(), calls=%async_computation.33 | async-start | bytes 5308416 | tf_op jit(solution)/shard_map/while/body/eval_jaxpr/reduce_scatter | solution.py:44
  1436.5 168.6 %all-gather.29.cloned.1.call-start = ((), (), s32[]{:S(2)}) async-start(), calls=%async_computation.34 | async-start | bytes 2654208 | tf_op jit(solution)/shard_map/while/body/eval_jaxpr/all_gather | solution.py:40
  1555.9 153.7 %reduce-scatter.58.cloned.1.call-start = ((), (), s32[]{:S(2)}) async-start(), calls=%async_computation.35 | async-start | bytes 5308416 | tf_op jit(solution)/shard_map/while/body/eval_jaxpr/reduce_scatter | solution.py:44
  1615.3 148.6 %all-gather.31.cloned.1.call-start = ((), (), s32[]{:S(2)}) async-start(), calls=%async_computation.36 | async-start | bytes 2654208 | tf_op jit(solution)/shard_map/while/body/eval_jaxpr/all_gather | solution.py:48
  1712.3 157.7 %reduce-scatter.60.cloned.1.call-start = ((), (), s32[]{:S(2)}) async-start(), calls=%async_computation.37 | async-start | bytes 5308416 | tf_op jit(solution)/shard_map/while/body/eval_jaxpr/reduce_scatter | solution.py:52
  1775.7 169.7 %all-gather.33.cloned.1.call-start = ((), (), s32[]{:S(2)}) async-start(), calls=%async_computation.38 | async-start | bytes 2654208 | tf_op jit(solution)/shard_map/while/body/eval_jaxpr/all_gather | solution.py:48
  1896.2 155.4 %reduce-scatter.62.cloned.1.call-start = ((), (), s32[]{:S(2)}) async-start(), calls=%async_computation.39 | async-start | bytes 5308416 | tf_op jit(solution)/shard_map/while/body/eval_jaxpr/reduce_scatter | solution.py:282
  1957.3 149.9 %all-gather.35.cloned.1.call-start = ((), (), s32[]{:S(2)}) async-start(), calls=%async_computation.40 | async-start | bytes 2654208 | tf_op jit(solution)/shard_map/while/body/eval_jaxpr/all_gather | solution.py:48
  2055.5 126.4 %reduce-scatter.66.cloned.1.call-start = ((), (), s32[]{:S(2)}) async-start(), calls=%async_computation.42 | async-start | bytes 663552 | tf_op jit(solution)/shard_map/while/body/eval_jaxpr/reduce_scatter | solution.py:285
  2063.1 206.9 %reduce-scatter.64.cloned.1.call-start = ((), (), s32[]{:S(2)}) async-start(), calls=%async_computation.41 | async-start | bytes 5308416 | tf_op jit(solution)/shard_map/while/body/eval_jaxpr/reduce_scatter | solution.py:52
  2307.7 105.3 %reduce-scatter.40.cloned.1.call-start = ((), (), s32[]{:S(2)}) async-start(), calls=%async_computation.23 | async-start | bytes 1474560
  2310.4 130.7 %reduce-scatter.42.cloned.1.call-start = ((), (), s32[]{:S(2)}) async-start(), calls=%async_computation.24 | async-start | bytes 1474560
  2311.9 157.4 %reduce-scatter.46.cloned.1.call-start = ((), (), s32[]{:S(2)}) async-start(), calls=%async_computation.26 | async-start | bytes 1474560
  2314.5 183.0 %reduce-scatter.48.cloned.1.call-start = ((), (), s32[]{:S(2)}) async-start(), calls=%async_computation.27 | async-start | bytes 1474560
  2315.9 209.6 %reduce-scatter.50.cloned.1.call-start = ((), (), s32[]{:S(2)}) async-start(), calls=%async_computation.28 | async-start | bytes 1474560
  2317.5 285.8 %all-reduce.15.cloned.1.call-start = ((), (), s32[]{:S(2)}) async-start(), calls=%async_computation.19 | async-start | bytes 7077888 | tf_op jit(solution)/shard_map/psum | solution.py:442
  2318.1 325.1 %reduce-scatter.34.cloned.1.call-start = ((), (), s32[]{:S(2)}) async-start(), calls=%async_computation.20 | async-start | bytes 3686400 | tf_op jit(solution)/shard_map/reduce_scatter | solution.py:426
  2321.7 361.1 %reduce-scatter.36.cloned.1.call-start = ((), (), s32[]{:S(2)}) async-start(), calls=%async_computation.21 | async-start | bytes 3686400 | tf_op jit(solution)/shard_map/reduce_scatter | solution.py:429
  (213 other events, 4614.2 us)
Sparse Core Ops, SparseCore 0:
  111.5 48.7 all-gather.24
  174.8 94.1 reduce-scatter.53
  271.1 52.4 all-gather.26
  331.0 94.3 reduce-scatter.55
  450.8 49.0 all-gather.28
  510.1 94.1 reduce-scatter.57
  607.2 51.4 all-gather.30
  670.5 94.1 reduce-scatter.59
  791.1 49.0 all-gather.32
  852.1 94.1 reduce-scatter.61
  950.4 51.4 all-gather.34
  1005.1 61.2 reduce-scatter.65
  1069.8 94.6 reduce-scatter.63
  1215.5 50.4 all-gather.24
  1280.5 94.1 reduce-scatter.53
  1376.8 52.4 all-gather.26
  1436.6 94.2 reduce-scatter.55
  1556.1 49.0 all-gather.28
  1615.4 94.1 reduce-scatter.57
  1712.4 51.4 all-gather.30
  1775.8 94.1 reduce-scatter.59
  1896.3 49.0 all-gather.32
  1957.4 94.1 reduce-scatter.61
  2055.7 51.4 all-gather.34
  2110.3 61.2 reduce-scatter.65
  2175.3 94.6 reduce-scatter.63
  2330.7 25.7 reduce-scatter.51
  2359.1 25.6 reduce-scatter.37
  2415.4 25.6 reduce-scatter.41
  2528.3 74.8 all-reduce.14
  2606.4 36.7 reduce-scatter.33
  2646.1 36.6 reduce-scatter.35
  (7 shorter events, 170.5 us)
where the time goes:
time: 2700 us; the launch traced here: 2690 us
  waiting for transfers between devices  1960 us (73%)
  blocking collectives  298 us (11%)
  matrix products  257 us (10%)
  local copies, waits for them, and re-layouts  92 us (3%)
  other arithmetic  67.7 us (3%)
    reduce_scatter x6, waiting for transfers between devices, reduce_cols(): return lax.psum_scatter(partial_sum, 'col', scatter_dimension=1, tiled=True)  566 us
    reduce_scatter x4, waiting for transfers between devices, reduce_grads(): return lax.psum_scatter(partial_sum, 'col', scatter_dimension=1, tiled=True)  349 us
    all_gather x6, waiting for transfers between devices, gather_grads(): return lax.all_gather(gradient, 'col', axis=1, tiled=True)  290 us
    all_gather x4, waiting for transfers between devices, gather_cols(): return lax.all_gather(modulated, 'col', axis=1, tiled=True)  198 us
    reduce_scatter x2, waiting for transfers between devices, micro_step(): lax.psum_scatter(matmul_nt(dquery_c, cquery_full), 'col', scatter_dimensi...  189 us
    unnamed x21, waiting for transfers between devices  178 us
    psum x8, blocking collectives, token_sums(): lax.psum((jnp.sum(first_in, axis=-1), jnp.sum(second_in, axis=-1)), 'col')  162 us
    psum x1, waiting for transfers between devices, shards(): lax.psum((sum_qbias, sum_vbias, sum_obias, sum_cqbias, sum_cvbias, sum_co...  75.9 us
  transfers between devices with their start and end apart: 39, of which 34 were waited for; matrix products, arithmetic and copies ran while one was open for 8% of the time, Pallas kernels for 0%

commit v1 on v0

v1 whole, which is shorter than its diff:
```python
import jax
import jax.numpy as jnp
from jax import lax
from jax.sharding import PartitionSpec as P

D = 1152
HEADS = 16
HD = 72

NORM_EPS = 1e-06
MASK_FILL = -1e30
BF = jnp.bfloat16
F32 = jnp.float32


def dot_nn(a, b):
    return lax.dot_general(a, b, (((1,), (0,)), ((), ())), preferred_element_type=F32)


def dot_tn(a, b):
    return lax.dot_general(a, b, (((0,), (0,)), ((), ())), preferred_element_type=F32)


def dot_nt(a, b):
    return lax.dot_general(a, b, (((1,), (1,)), ((), ())), preferred_element_type=F32)


def after(value, *deps):
    return lax.optimization_barrier((value,) + deps)[0]


def bit_reverse(value, bits):
    out = 0
    for b in range(bits):
        out = out | (((value >> b) & 1) << (bits - 1 - b))
    return out


def row_swap(value, rows, bit):
    return lax.ppermute(value, "row", [(i, i ^ bit) for i in range(rows)])


def col_swap(value, cols, mask):
    return lax.ppermute(value, "col", [(i, i ^ mask) for i in range(cols)])


def layer_norm(resid):
    mean = jnp.mean(resid, axis=0, keepdims=True)
    centered = resid - mean
    var = jnp.mean(centered * centered, axis=0, keepdims=True)
    inv = lax.rsqrt(var + NORM_EPS)
    return centered * inv, inv


def norm_backward(grad, normed, inv, scale):
    dn = grad * (1.0 + scale)
    first = jnp.mean(dn, axis=0, keepdims=True)
    second = jnp.mean(dn * normed, axis=0, keepdims=True)
    back = (dn - first - normed * second) * inv
    return back, jnp.sum(grad, axis=1), jnp.sum(grad * normed, axis=1)


def attend_forward(q_t, k_t, v_t, valid):
    heads = q_t.shape[0] // HD
    q3, k3, v3 = (a.reshape(heads, HD, a.shape[1]) for a in (q_t, k_t, v_t))
    s = jnp.einsum("hdk,hdq->hkq", k3, q3, preferred_element_type=F32) * HD ** -0.5
    if valid is not None:
        s = jnp.where(valid[None, :, None], s, MASK_FILL)
    top = jnp.max(s, axis=1, keepdims=True)
    lse = top + jnp.log(jnp.sum(jnp.exp(s - top), axis=1, keepdims=True))
    p = jnp.exp(s - lse).astype(BF)
    out = jnp.einsum("hdk,hkq->hdq", v3, p, preferred_element_type=F32)
    return out.reshape(q_t.shape).astype(BF), lse


def attend_backward(q_t, k_t, v_t, valid, lse, do_t):
    heads = q_t.shape[0] // HD
    q3, k3, v3, do3 = (a.reshape(heads, HD, a.shape[1]) for a in (q_t, k_t, v_t, do_t))
    s = jnp.einsum("hdk,hdq->hkq", k3, q3, preferred_element_type=F32) * HD ** -0.5
    if valid is not None:
        s = jnp.where(valid[None, :, None], s, MASK_FILL)
    p = jnp.exp(s - lse)
    dv = jnp.einsum("hdq,hkq->hdk", do3, p.astype(BF), preferred_element_type=F32)
    dp = jnp.einsum("hdk,hdq->hkq", v3, do3, preferred_element_type=F32)
    ds = p * (dp - jnp.sum(dp * p, axis=1, keepdims=True))
    ds = (ds * HD ** -0.5).astype(BF)
    dq = jnp.einsum("hdk,hkq->hdq", k3, ds, preferred_element_type=F32)
    dk = jnp.einsum("hdq,hkq->hdk", q3, ds, preferred_element_type=F32)
    return dq.reshape(q_t.shape).astype(BF), dk.reshape(k_t.shape).astype(BF), dv.reshape(k_t.shape).astype(BF)


def shards(
    block_input,
    text_tokens,
    text_length,
    time_index,
    shift_table,
    time_table,
    query_weight,
    key_weight,
    value_weight,
    query_bias,
    value_bias,
    out_weight,
    out_bias,
    cross_query,
    cross_key,
    cross_value,
    cross_query_bias,
    cross_value_bias,
    cross_out,
    cross_out_bias,
    up_weight,
    up_bias,
    down_weight,
    down_bias,
    out_grad,
):
    rows, cols = lax.axis_size("row"), lax.axis_size("col")
    r, c = lax.axis_index("row"), lax.axis_index("col")
    row_bits = rows.bit_length() - 1
    half = cols // 2
    feat = block_input.shape[1]
    chunk = D // rows
    width = 2 * block_input.shape[2] // cols
    texts = text_tokens.shape[1]
    steps = time_table.shape[2]
    ups = up_bias.shape[0]
    core, low_z, micro = r & 1, (c >> 1) & 1, c // half
    home_row = (r - core) | low_z
    at_home = core == low_z
    r_rev = bit_reverse(r, row_bits)

    kv_masks = [1 << b for b in range(2, cols.bit_length() - 2)]
    swap_pairs = []
    for i in range(rows):
        for j in range(cols):
            swap_pairs.append(
                (i * cols + j, ((i & ~1) | ((j >> 1) & 1)) * cols + ((j & ~2) | ((i & 1) << 1)))
            )

    def place_swap(value):
        return lax.ppermute(value, ("row", "col"), swap_pairs)

    def to_local(value):
        parts = value.reshape((rows, chunk) + value.shape[1:])
        picked = [
            lax.dynamic_index_in_dim(parts, r ^ bit_reverse(i, row_bits), 0, keepdims=False)
            for i in range(rows)
        ]
        return jnp.concatenate(picked, axis=0)

    def to_natural(value):
        parts = value.reshape((rows, chunk) + value.shape[1:])
        picked = [
            lax.dynamic_index_in_dim(parts, r_rev ^ bit_reverse(i, row_bits), 0, keepdims=False)
            for i in range(rows)
        ]
        return jnp.concatenate(picked, axis=0)

    def tokens_in(value):
        blocks = value.reshape(2, feat, half, width).transpose(0, 2, 1, 3).reshape(cols, feat, width)
        blocks = lax.all_to_all(blocks, "col", 0, 0, tiled=True)
        return to_local(place_swap(blocks.reshape(D, width)))

    def tokens_out(value):
        blocks = place_swap(to_natural(value.astype(BF))).reshape(cols, feat, width)
        blocks = lax.all_to_all(blocks, "col", 0, 0, tiled=True)
        blocks = blocks.reshape(2, half, feat, width).transpose(0, 2, 1, 3)
        return blocks.reshape(2, feat, half * width).astype(F32)

    def gather_pair(value):
        return jnp.concatenate([value, col_swap(value, cols, 1)], axis=1)

    def reduce_pair(value):
        own, other = value[:, :width], value[:, width:]
        return own + col_swap(other.astype(BF), cols, 1).astype(F32)

    def gather_keys(value):
        parts = [value]
        parts = parts + [row_swap(p, rows, 1) for p in parts]
        for mask in kv_masks:
            parts = parts + [col_swap(p, cols, mask) for p in parts]
        return jnp.concatenate(parts, axis=1)

    def reduce_keys(value):
        for mask in reversed(kv_masks):
            h = value.shape[1] // 2
            value = (value[:, :h].astype(F32) + col_swap(value[:, h:], cols, mask).astype(F32)).astype(BF)
        h = value.shape[1] // 2
        return (value[:, :h].astype(F32) + row_swap(value[:, h:], rows, 1).astype(F32)).astype(BF)

    row_order = [1 << b for b in reversed(range(row_bits))]

    def gather_weights(shards_w, gate):
        sizes = [w.shape[1] for w in shards_w]
        flat = jnp.concatenate(shards_w, axis=1) if len(shards_w) > 1 else shards_w[0]
        if gate is not None:
            flat = after(flat, gate)
        near = [flat] + [col_swap(flat, cols, e << 1) for e in range(1, half)]
        z_gate = near[-1]
        pieces, start = [], 0
        for size in sizes:
            pieces += [p[:, start : start + size] for p in near]
            start += size
        parts = [jnp.concatenate(pieces, axis=1)]
        for bit in row_order:
            parts = parts + [row_swap(p, rows, bit) for p in parts]
        full = jnp.concatenate(parts, axis=0)
        out, start = [], 0
        for size in sizes:
            out.append(full[:, start : start + size * half])
            start += size * half
        return full, out, z_gate

    def reduce_weights(left, right, sizes):
        end = D
        received = []
        for bit in reversed(row_order):
            start = end // 2
            part = dot_nt(left[start:end], right)
            for piece in received:
                part = part + piece[start:end].astype(F32)
            received.append(row_swap(part.astype(BF), rows, bit))
            end = start
        own = dot_nt(left[:end], right)
        for piece in received:
            own = own + piece[:end].astype(F32)
        groups, start = [], 0
        for size in sizes:
            groups.append([own[:, start + e * size : start + (e + 1) * size] for e in range(half)])
            start += size * half
        total = jnp.concatenate([g[0] for g in groups], axis=1) if len(groups) > 1 else groups[0][0]
        for e in range(1, half):
            sent = [g[e].astype(BF) for g in groups]
            sent = jnp.concatenate(sent, axis=1) if len(sent) > 1 else sent[0]
            total = total + col_swap(sent, cols, e << 1).astype(F32)
        out, start = [], 0
        for size in sizes:
            out.append(total[:, start : start + size])
            start += size
        return out

    qkv_w, _, gate_one = gather_weights([query_weight, key_weight, value_weight], None)
    _, (out_w, cq_w, ck_w, cv_w, cout_w), gate_two = gather_weights(
        [out_weight.T, cross_query, cross_key, cross_value, cross_out.T], gate_one
    )
    up_w, _, gate_three = gather_weights([up_weight], gate_two)
    down_w, _, _ = gather_weights([down_weight.T], gate_three)

    lengths_steps = lax.all_gather(jnp.stack([text_length[:, 0], time_index[:, 0]]), "row")
    length = lengths_steps[home_row, 0, micro]
    step_all = lengths_steps[:, 1, :].T.reshape(2 * rows)
    step_ids = jnp.arange(steps, dtype=jnp.int32)
    onehot = (time_index[:, 0][:, None] == step_ids[None, :]).astype(F32)
    modulation = lax.dot_general(
        onehot,
        time_table.reshape(6 * feat, steps),
        (((1,), (1,)), ((), ())),
        precision=lax.Precision.HIGHEST,
        preferred_element_type=F32,
    ).reshape(2, 6, feat) + shift_table[None]
    small = jnp.concatenate(
        [
            modulation.reshape(12, feat),
            out_bias[None],
            cross_out_bias[None],
            down_bias[None],
            query_bias[None],
            value_bias[None],
            cross_query_bias[None],
            cross_value_bias[None],
            up_bias.reshape(ups // feat, feat),
        ],
        axis=0,
    )
    small = lax.all_gather(small, "col")
    mods = small[:, :12].transpose(1, 0, 2).reshape(2, 6, D)
    mods = lax.dynamic_index_in_dim(mods, micro, 0, keepdims=False)
    mods = jnp.where(at_home, mods, row_swap(mods, rows, 1))
    model_rows = jnp.concatenate([mods, small[:, 12:15].transpose(1, 0, 2).reshape(3, D)], axis=0)
    model_rows = to_local(model_rows.T)
    shift_a, scale_a, gate_a, shift_m, scale_m, gate_m, out_b, cout_b, down_b = (
        model_rows[:, i : i + 1] for i in range(9)
    )
    col_rows = [
        lax.dynamic_index_in_dim(small, c ^ (e << 1), 0, keepdims=False)[15:] for e in range(half)
    ]
    col_rows = jnp.stack(col_rows, axis=1)
    q_b, v_b, cq_b, cv_b = (col_rows[i].reshape(half * feat, 1) for i in range(4))
    up_b = col_rows[4:].transpose(1, 0, 2).reshape(half * ups, 1)

    text_blocks = text_tokens.transpose(0, 2, 1)
    text_t = lax.all_to_all(jnp.repeat(text_blocks, half, axis=0), "col", 0, 0, tiled=True).reshape(D, texts)
    text_t = to_local(jnp.where(at_home, text_t, row_swap(text_t, rows, 1)))
    valid = jnp.arange(texts, dtype=jnp.int32) < length

    resid = tokens_in(block_input).astype(F32)
    cot = tokens_in(out_grad).astype(F32)
    normed_a, inv_a = layer_norm(resid)
    attn_full = gather_pair((normed_a * (1.0 + scale_a) + shift_a).astype(BF))
    heads_w = half * feat
    qkv_bias = jnp.concatenate([q_b, jnp.zeros_like(q_b), v_b], axis=0)
    qkv = (dot_tn(qkv_w, attn_full) + qkv_bias).astype(BF)
    q_t = qkv[:heads_w]
    kv_t = gather_keys(qkv[heads_w:])
    k_t, v_t = kv_t[:heads_w], kv_t[heads_w:]
    att, lse = attend_forward(q_t, k_t, v_t, None)
    branch_a = reduce_pair(dot_nn(out_w, att)) + out_b
    after_attn = resid + gate_a * branch_a
    cross_full = gather_pair(after_attn.astype(BF))
    cq_t = (dot_tn(cq_w, cross_full) + cq_b).astype(BF)
    ck_t = dot_tn(ck_w, text_t).astype(BF)
    cv_t = (dot_tn(cv_w, text_t) + cv_b).astype(BF)
    catt, clse = attend_forward(cq_t, ck_t, cv_t, valid)
    after_cross = after_attn + reduce_pair(dot_nn(cout_w, catt)) + cout_b
    normed_m, inv_m = layer_norm(after_cross)
    mlp_full = gather_pair((normed_m * (1.0 + scale_m) + shift_m).astype(BF))
    hidden_pre = dot_tn(up_w, mlp_full) + up_b
    hidden_val, gelu_pull = jax.vjp(lambda v: jax.nn.gelu(v, approximate=True), hidden_pre)
    hidden = hidden_val.astype(BF)
    branch_m = reduce_pair(dot_nn(down_w, hidden)) + down_b
    block_output = tokens_out(after_cross + gate_m * branch_m)

    grad_mlp = gate_m * cot
    low_full = gather_pair(grad_mlp.astype(BF))
    g_down_b = jnp.sum(grad_mlp, axis=1)
    g_gate_m = jnp.sum(cot * branch_m, axis=1)
    grad_pre = gelu_pull(dot_tn(down_w, low_full))[0].astype(BF)
    (g_down,) = reduce_weights(low_full, hidden, [ups])
    back_in = reduce_pair(dot_nn(up_w, grad_pre))
    (g_up,) = reduce_weights(mlp_full, grad_pre, [ups])
    g_up_b = jnp.sum(grad_pre.astype(F32), axis=1)
    back_m, g_shift_m, g_scale_m = norm_backward(back_in, normed_m, inv_m, scale_m)
    grad_cross = cot + back_m
    g_cout_b = jnp.sum(grad_cross, axis=1)
    low_cross = gather_pair(grad_cross.astype(BF))
    dcatt = dot_tn(cout_w, low_cross).astype(BF)
    dcq, dck, dcv = attend_backward(cq_t, ck_t, cv_t, valid, clse, dcatt)
    g_cq_b = jnp.sum(dcq.astype(F32), axis=1)
    g_cv_b = jnp.sum(dcv.astype(F32), axis=1)
    grad_res = grad_cross + reduce_pair(dot_nn(cq_w, dcq))
    grad_text = to_natural(dot_nn(ck_w, dck) + dot_nn(cv_w, dcv)).astype(BF)
    grad_text = grad_text.astype(F32) + row_swap(grad_text, rows, 1).astype(F32)
    grad_text = jnp.where(at_home, grad_text, 0.0).astype(BF).reshape(cols, feat, texts)
    grad_text = lax.all_to_all(grad_text, "col", 0, 0, tiled=True)
    grad_text = jnp.sum(grad_text.reshape(2, half, feat, texts).astype(F32), axis=1).transpose(0, 2, 1)
    (g_cout,) = reduce_weights(low_cross, catt, [feat])
    (g_cq,) = reduce_weights(cross_full, dcq, [feat])
    g_ck, g_cv = reduce_weights(text_t, jnp.concatenate([dck, dcv], axis=0), [feat, feat])
    g_gate_a = jnp.sum(grad_res * branch_a, axis=1)
    grad_attn = gate_a * grad_res
    g_out_b = jnp.sum(grad_attn, axis=1)
    low_attn = gather_pair(grad_attn.astype(BF))
    datt = dot_tn(out_w, low_attn).astype(BF)
    dq, dk, dv = attend_backward(q_t, k_t, v_t, None, lse, datt)
    (g_out,) = reduce_weights(low_attn, att, [feat])
    dkv = reduce_keys(jnp.concatenate([dk, dv], axis=0))
    dqkv = jnp.concatenate([dq, dkv], axis=0)
    g_q, g_k, g_v = reduce_weights(attn_full, dqkv, [feat, feat, feat])
    g_q_b = jnp.sum(dq.astype(F32), axis=1)
    g_v_b = jnp.sum(dkv[heads_w:].astype(F32), axis=1)
    back_a, g_shift_a, g_scale_a = norm_backward(
        reduce_pair(dot_nn(qkv_w, dqkv)), normed_a, inv_a, scale_a
    )
    grad_input = tokens_out(grad_res + back_a)

    model_g = jnp.stack(
        [g_shift_a, g_scale_a, g_gate_a, g_shift_m, g_scale_m, g_gate_m, g_out_b, g_cout_b, g_down_b], axis=1
    )
    model_g = to_natural(model_g).T.reshape(9, cols, feat).transpose(1, 0, 2)
    per_col = ups // feat
    col_g = jnp.concatenate(
        [g.reshape(half, 1, feat) for g in (g_q_b, g_v_b, g_cq_b, g_cv_b)] + [g_up_b.reshape(half, per_col, feat)],
        axis=1,
    )
    side = c & 1
    blocks = []
    for j in range(cols):
        part = lax.dynamic_index_in_dim(col_g, (j >> 1) ^ (c >> 1), 0, keepdims=False)
        blocks.append(jnp.where(side == (j & 1), part, 0.0))
    small_g = jnp.concatenate([model_g, jnp.stack(blocks)], axis=1)
    small_g = lax.all_to_all(small_g, "col", 0, 0, tiled=True)
    mod_g = small_g[:, :6].reshape(2, cols // 8, 2, 2, 6, feat).sum(axis=(1, 3))
    bias_g = small_g[:, 6:].sum(axis=0)
    small_g = lax.all_gather(jnp.concatenate([mod_g.reshape(24, feat), bias_g], axis=0), "row")
    mod_g = small_g[:, :24].reshape(rows // 2, 2, 2, 2, 6, feat).sum(axis=1)
    mod_g = mod_g.transpose(1, 0, 2, 3, 4).reshape(2 * rows, 6, feat)
    bias_g = small_g[:, 24:].sum(axis=0)
    g_shift = mod_g.sum(axis=0)
    onehot_all = (step_all[:, None] == step_ids[None, :]).astype(F32)
    g_time = lax.dot_general(
        mod_g.reshape(2 * rows, 6 * feat),
        onehot_all,
        (((0,), (0,)), ((), ())),
        precision=lax.Precision.HIGHEST,
        preferred_element_type=F32,
    ).reshape(6, feat, steps)
    g_out_b, g_cout_b, g_down_b, g_q_b, g_v_b, g_cq_b, g_cv_b = (bias_g[i] for i in range(7))
    g_up_b = bias_g[7:].reshape(ups)
    return (
        block_output,
        grad_input,
        grad_text,
        g_shift,
        g_time,
        g_q,
        g_k,
        g_v,
        g_q_b,
        g_v_b,
        g_out.T,
        g_out_b,
        g_cq,
        g_ck,
        g_cv,
        g_cq_b,
        g_cv_b,
        g_cout.T,
        g_cout_b,
        g_up,
        g_up_b,
        g_down.T,
        g_down_b,
    )


def solution(mesh):
    return jax.shard_map(
        shards,
        mesh=mesh,
        in_specs=(
            P(None, "col", "row"),
            P(None, "row", "col"),
            P(None, "row"),
            P(None, "row"),
            P(None, "col"),
            P(None, "col", None),
            P("row", "col"),
            P("row", "col"),
            P("row", "col"),
            P("col"),
            P("col"),
            P("col", "row"),
            P("col"),
            P("row", "col"),
            P("row", "col"),
            P("row", "col"),
            P("col"),
            P("col"),
            P("col", "row"),
            P("col"),
            P("row", "col"),
            P("col"),
            P("col", "row"),
            P("col"),
            P(None, "col", "row"),
        ),
        out_specs=(
            P(None, "col", "row"),
            P(None, "col", "row"),
            P(None, "row", "col"),
            P(None, "col"),
            P(None, "col", None),
            P("row", "col"),
            P("row", "col"),
            P("row", "col"),
            P("col"),
            P("col"),
            P("col", "row"),
            P("col"),
            P("row", "col"),
            P("row", "col"),
            P("row", "col"),
            P("col"),
            P("col"),
            P("col", "row"),
            P("col"),
            P("row", "col"),
            P("col"),
            P("col", "row"),
            P("col"),
        ),
        check_vma=False,
    )
```

time: 2700 us -> 853 us (0.32)
  waiting for transfers between devices: 1960 us -> 266 us
  blocking collectives: 298 us -> 68.1 us
  starting transfers between devices: 2.06 us -> 138 us
  matrix products: 257 us -> 210 us
    reduce_scatter x16 -> x0, waiting for transfers between devices: 1180 us -> none  [the longest x6 566 us: reduce_cols(): return lax.psum_scatter(partial_sum, 'col', scatter_dimension=1, tiled=True)]
    all_gather x14 -> x0, waiting for transfers between devices: 518 us -> none  [the longest x6 290 us: gather_grads(): return lax.all_gather(gradient, 'col', axis=1, tiled=True)]
    ppermute x0 -> x80, waiting for transfers between devices: none -> 246 us  [the longest x45 191 us: col_swap(): return lax.ppermute(value, 'col', [(i, i ^ mask) for i in range(cols)])]
    unnamed x21 -> x0, waiting for transfers between devices: 178 us -> none
    psum x9 -> x0, blocking collectives: 173 us -> none  [the longest x8 162 us: token_sums(): lax.psum((jnp.sum(first_in, axis=-1), jnp.sum(second_in, axis=-1)), 'col')]
    ppermute x0 -> x80, starting transfers between devices: none -> 104 us  [the longest x45 63.4 us: col_swap(): return lax.ppermute(value, 'col', [(i, i ^ mask) for i in range(cols)])]
    psum x1 -> x0, waiting for transfers between devices: 75.9 us -> none  [shards(): lax.psum((sum_qbias, sum_vbias, sum_obias, sum_cqbias, sum_cvbias, sum_co...]
    all_gather x10 -> x3, blocking collectives: 125 us -> 68.1 us  [the longest x1 42.4 us: shards(): small = lax.all_gather(small, 'col')]
  transfers between devices with their start and end apart: 39 -> 87, of which waited for: 34 -> 30; matrix products, arithmetic and copies ran while one was open for 8% -> 38% of each run, Pallas kernels for 0% -> 0%
where the time goes in v1:
time: 853 us; the launch traced here: 838 us
  waiting for transfers between devices  266 us (31%)
  matrix products  210 us (25%)
  starting transfers between devices  138 us (16%)
  local copies, waits for them, and re-layouts  92.1 us (11%)
  blocking collectives  68.1 us (8%)
  other arithmetic  60.3 us (7%)
    ppermute x45, waiting for transfers between devices, col_swap(): return lax.ppermute(value, 'col', [(i, i ^ mask) for i in range(cols)])  191 us
    ppermute x45, starting transfers between devices, col_swap(): return lax.ppermute(value, 'col', [(i, i ^ mask) for i in range(cols)])  63.4 us
    ppermute x31, waiting for transfers between devices, row_swap(): return lax.ppermute(value, 'row', [(i, i ^ bit) for i in range(rows)])  55.8 us
    dot_general x21, matrix products, dot_nt(): lax.dot_general(a, b, (((1,), (1,)), ((), ())), preferred_element_type=F32)  55.7 us
    all_gather x1, blocking collectives, shards(): small = lax.all_gather(small, 'col')  42.4 us
    dot_general x8, matrix products, dot_tn(): lax.dot_general(a, b, (((0,), (0,)), ((), ())), preferred_element_type=F32)  31.3 us
    dot_general x8, matrix products, dot_nn(): lax.dot_general(a, b, (((1,), (0,)), ((), ())), preferred_element_type=F32)  26.7 us
    dot_general x2, matrix products, attend_backward(): dq = jnp.einsum('hdk,hkq->hdq', k3, ds, preferred_element_type=F32)  26.6 us
  transfers between devices with their start and end apart: 87, of which 30 were waited for; matrix products, arithmetic and copies ran while one was open for 38% of the time, Pallas kernels for 0%

profile of v1, /device:TPU:0, one launch (start us, length us, event | category | flops | bytes accessed | tf_op | source)
XLA Modules:
  0.0 838.3 jit_solution(13292796607015781618)
XLA Ops:
  18.1 42.4 %all-gather.3 = f32[8,23,144]{2,1,0:T(8,128)S(1)} all-gather(f32[1,23,144]{2,1,0:T(8,128)S(1)} %bitcast.293), channel_id=2, replica_groups=mesh['row'=4,'col'=8] {'col'}, dimensions={0}, use_global_device_ids=true | all-gather | bytes 119232 | tf_op jit(solution)/shard_map/all_gather | solution.py:277
  76.6 7.4 all-to-all-done
  91.8 8.7 %collective-permute-done.11 = bf16[288,1728]{1,0:T(8,128)(2,1)} collective-permute-done((bf16[288,1728]{1,0:T(8,128)(2,1)}, bf16[288,1728]{1,0:T(8,128)(2,1)}, u32[]{:S(2)}, u32[]{:S(2)}) %collective-permute-start.11) | collective-permute-done | bytes 995360 | tf_op jit(solution)/shard_map/ppermute | solution.py:40
  100.5 6.9 collective-permute-start.13
  108.3 19.4 %collective-permute-done.4 = bf16[288,720]{1,0:T(8,128)(2,1)S(1)} collective-permute-done((bf16[288,720]{1,0:T(8,128)(2,1)S(1)}, bf16[288,720]{1,0:T(8,128)(2,1)S(1)}, u32[]{:S(2)}, u32[]{:S(2)}) %collective-permute-start.4) | collective-permute-done | bytes 414752 | tf_op jit(solution)/shard_map/ppermute | solution.py:44
  154.8 20.1 %all-gather.4 = s32[4,2,2]{2,1,0:T(2,128)S(1)} all-gather(s32[1,2,2]{2,1,0:T(2,128)S(1)} %add_bitcast_fusion), channel_id=3, replica_groups=mesh['row'=4,'col'=8] {'row'}, dimensions={0}, use_global_device_ids=true | all-gather | bytes 80 | tf_op jit(solution)/shard_map/all_gather | solution.py:251
  184.6 8.2 multiply_reduce_fusion.1
  192.8 8.5 %exponential_reduce_fusion = f32[8,512]{1,0:T(8,128)S(1)} fusion(f32[8,1024,512]{2,1,0:T(8,128)} %get-tuple-element.310, f32[8,512]{1,0:T(8,128)S(1)} %get-tuple-element.309), kind=kLoop, calls=%fused_computation.6 | loop fusion | flops 12578816 | bytes 16809984 | tf_op jit(solution)/shard_map/reduce_sum | solution.py:70
  201.3 8.7 %convolution_convert_fusion.11 = bf16[8,72,512]{2,1,0:T(8,128)(2,1)S(1)} fusion(bf16[8,72,1024]{2,1,0:T(8,128)(2,1)S(1)} %bitcast.233, f32[8,512]{1,0:T(8,128)S(1)} %log_add_fusion.1, f32[8,1024,512]{2,1,0:T(8,128)} %get-tuple-element.310), kind=kOutput, calls=%fused_computation.121 | convolution fusion | flops 616857600 | bytes 18563072 | tf_op jit(solution)/shard_map/hdk,hkq->hdq/dot_general | solution.py:72
  224.3 8.7 %collective-permute-done.16 = bf16[1152,256]{1,0:T(8,128)(2,1)S(1)} collective-permute-done((bf16[1152,256]{1,0:T(8,128)(2,1)S(1)}, bf16[1152,256]{1,0:T(8,128)(2,1)S(1)}, u32[]{:S(2)}, u32[]{:S(2)}) %collective-permute-start.16) | collective-permute-done | bytes 589856 | tf_op jit(solution)/shard_map/ppermute | solution.py:44
  248.3 14.5 %concatenate.155 = bf16[288,2304]{1,0:T(8,128)(2,1)} concatenate(bf16[288,576]{1,0:T(8,128)(2,1)S(1)} %copy-done.99, bf16[288,576]{1,0:T(8,128)(2,1)} %copy-done.101, bf16[288,576]{1,0:T(8,128)(2,1)} %copy-done.100, bf16[288,576]{1,0:T(8,128)(2,1)} %collective-permute-done.20), dimensions={1} | concatenate | bytes 2654208 | tf_op jit(solution)/shard_map/concatenate | solution.py:206
  280.9 6.9 collective-permute-start.22
  289.9 23.6 %collective-permute-done.22 = bf16[288,576]{1,0:T(8,128)(2,1)} collective-permute-done((bf16[288,576]{1,0:T(8,128)(2,1)}, bf16[288,576]{1,0:T(8,128)(2,1)}, u32[]{:S(2)}, u32[]{:S(2)}) %collective-permute-start.22) | collective-permute-done | bytes 331808 | tf_op jit(solution)/shard_map/ppermute | solution.py:44
  331.0 23.9 %collective-permute-done.24 = bf16[288,2304]{1,0:T(8,128)(2,1)S(1)} collective-permute-done((bf16[288,2304]{1,0:T(8,128)(2,1)}, bf16[288,2304]{1,0:T(8,128)(2,1)S(1)}, u32[]{:S(2)}, u32[]{:S(2)}) %collective-permute-start.24) | collective-permute-done | bytes 1327136 | tf_op jit(solution)/shard_map/ppermute | solution.py:40
  356.6 6.8 multiply_convert_fusion.1
  363.5 7.5 collective-permute-done.36
  377.8 7.5 fusion.117
  399.3 8.1 collective-permute-done.33
  407.3 11.3 %collective-permute-done.37 = bf16[1152,256]{1,0:T(8,128)(2,1)} collective-permute-done((bf16[1152,256]{1,0:T(8,128)(2,1)}, bf16[1152,256]{1,0:T(8,128)(2,1)}, u32[]{:S(2)}, u32[]{:S(2)}) %collective-permute-start.37) | collective-permute-done | bytes 589856 | tf_op jit(solution)/shard_map/ppermute | solution.py:44
  476.6 8.0 collective-permute-done.39
  515.8 12.0 %all-to-all-done.2 = bf16[8,144,256]{2,1,0:T(8,128)(2,1)} async-done(((bf16[8,144,256]{2,1,0:T(8,128)(2,1)}), bf16[8,144,256]{2,1,0:T(8,128)(2,1)}, u32[]{:S(2)}, u32[]{:S(2)}) %all-to-all-start.2) | async-done | bytes 589856 | tf_op jit(solution)/shard_map/all_to_all | solution.py:168
  546.0 8.2 fusion.289
  554.2 23.3 %convert_reduce_fusion.4 = (f32[8,72]{1,0:T(8,128)S(1)}, bf16[8,72,512]{2,1,0:T(8,128)(2,1)}) fusion(bf16[8,72,1024]{2,1,0:T(8,128)(2,1)S(1)} %bitcast.248, f32[8,1024,512]{2,1,0:T(8,128)} %fusion.289, f32[8,512]{1,0:T(8,128)S(1)} %copy-done.114, f32[8,1024,512]{2,1,0:T(8,128)} %get-tuple-element.310), kind=kOutput, calls=%fused_computation.187 | convolution fusion | flops 642617792 | bytes 35342592 | tf_op jit(solution)/shard_map/hdk,hkq->hdq/dot_general | solution.py:87
  577.5 23.3 %fusion.38 = bf16[8,72,1024]{2,1,0:T(8,128)(2,1)S(1)} fusion(bf16[8,72,512]{2,1,0:T(8,128)(2,1)S(1)} %bitcast.268, f32[8,1024,512]{2,1,0:T(8,128)} %fusion.289, f32[8,512]{1,0:T(8,128)S(1)} %copy-done.114, f32[8,1024,512]{2,1,0:T(8,128)} %get-tuple-element.310), kind=kOutput, calls=%fused_computation.71 | convolution fusion | flops 642323456 | bytes 35340288 | tf_op jit(solution)/shard_map/hdq,hkq->hdk/dot_general | solution.py:88
  604.0 8.9 %convolution_convert_fusion.4 = bf16[8,72,1024]{2,1,0:T(8,128)(2,1)S(1)} fusion(bf16[8,72,512]{2,1,0:T(8,128)(2,1)} %bitcast.266, f32[8,512]{1,0:T(8,128)S(1)} %copy-done.114, f32[8,1024,512]{2,1,0:T(8,128)} %get-tuple-element.310), kind=kOutput, calls=%fused_computation.72 | convolution fusion | flops 617152512 | bytes 18563072 | tf_op jit(solution)/shard_map/hdq,hkq->hdk/dot_general | solution.py:83
  627.1 7.5 collective-permute-done.61
  640.7 11.5 %collective-permute-done.63 = bf16[288,288]{1,0:T(8,128)(2,1)S(1)} collective-permute-done((bf16[288,288]{1,0:T(8,128)(2,1)S(1)}, bf16[288,288]{1,0:T(8,128)(2,1)S(1)}, u32[]{:S(2)}, u32[]{:S(2)}) %collective-permute-start.63) | collective-permute-done | bytes 165920 | tf_op jit(solution)/shard_map/ppermute | solution.py:44
  697.7 14.2 %collective-permute-done.71 = bf16[288,2304]{1,0:T(8,128)(2,1)} collective-permute-done((bf16[288,2304]{1,0:T(8,128)(2,1)}, bf16[288,2304]{1,0:T(8,128)(2,1)}, u32[]{:S(2)}, u32[]{:S(2)}) %collective-permute-start.71) | collective-permute-done | bytes 1327136 | tf_op jit(solution)/shard_map/ppermute | solution.py:40
  746.2 6.9 all-to-all-start.4
  765.3 12.4 %collective-permute-done.74 = bf16[288,576]{1,0:T(8,128)(2,1)} collective-permute-done((bf16[288,576]{1,0:T(8,128)(2,1)}, bf16[288,576]{1,0:T(8,128)(2,1)}, u32[]{:S(2)}, u32[]{:S(2)}) %collective-permute-start.74) | collective-permute-done | bytes 331808 | tf_op jit(solution)/shard_map/ppermute | solution.py:44
  777.7 23.0 %collective-permute-done.73 = bf16[288,576]{1,0:T(8,128)(2,1)S(1)} collective-permute-done((bf16[288,576]{1,0:T(8,128)(2,1)}, bf16[288,576]{1,0:T(8,128)(2,1)S(1)}, u32[]{:S(2)}, u32[]{:S(2)}) %collective-permute-start.73) | collective-permute-done | bytes 331808 | tf_op jit(solution)/shard_map/ppermute | solution.py:44
  813.0 16.3 %collective-permute-done.48 = bf16[288,432]{1,0:T(8,128)(2,1)S(1)} collective-permute-done((bf16[288,432]{1,0:T(8,128)(2,1)S(1)}, bf16[288,432]{1,0:T(8,128)(2,1)S(1)}, u32[]{:S(2)}, u32[]{:S(2)}) %collective-permute-start.48) | collective-permute-done | bytes 248864 | tf_op jit(solution)/shard_map/ppermute | solution.py:44
  (728 shorter events, 409.8 us)
Async XLA Ops:
  7.8 61.3 %collective-permute-start.10 = (bf16[288,432]{1,0:T(8,128)(2,1)}, bf16[288,432]{1,0:T(8,128)(2,1)}, u32[]{:S(2)}, u32[]{:S(2)}) collective-permute-start(bf16[288,432]{1,0:T(8,128)(2,1)} %pad_maximum_fusion.33), channel_id=1, source_target_pairs={{0,4},{1,5},{2,6},{3,7},{4,0},{5,1},{6,2},{7,3},{8,12},{9,13},{10,... | collective-permute-start | bytes 746504 | tf_op jit(solution)/shard_map/ppermute | solution.py:44
  11.8 58.4 %collective-permute-start.9 = (bf16[288,432]{1,0:T(8,128)(2,1)}, bf16[288,432]{1,0:T(8,128)(2,1)}, u32[]{:S(2)}, u32[]{:S(2)}) collective-permute-start(bf16[288,432]{1,0:T(8,128)(2,1)} %pad_maximum_fusion.33), channel_id=1, source_target_pairs={{0,2},{1,3},{2,0},{3,1},{4,6},{5,7},{6,4},{7,5},{8,10},{9,11},{10,... | collective-permute-start | bytes 746504 | tf_op jit(solution)/shard_map/ppermute | solution.py:44
  13.4 58.1 %collective-permute-start.2 = (bf16[288,432]{1,0:T(8,128)(2,1)}, bf16[288,432]{1,0:T(8,128)(2,1)}, u32[]{:S(2)}, u32[]{:S(2)}) collective-permute-start(bf16[288,432]{1,0:T(8,128)(2,1)} %pad_maximum_fusion.33), channel_id=1, source_target_pairs={{0,6},{1,7},{2,4},{3,5},{4,2},{5,3},{6,0},{7,1},{8,14},{9,15},{10,... | collective-permute-start | bytes 746504 | tf_op jit(solution)/shard_map/ppermute | solution.py:44
  86.5 44.8 %collective-permute-start.5 = (bf16[288,720]{1,0:T(8,128)(2,1)S(1)}, bf16[288,720]{1,0:T(8,128)(2,1)S(1)}, u32[]{:S(2)}, u32[]{:S(2)}) collective-permute-start(bf16[288,720]{1,0:T(8,128)(2,1)S(1)} %concatenate.142), channel_id=1, source_target_pairs={{0,6},{1,7},{2,4},{3,5},{4,2},{5,3},{6,0},{7,1},{8,14},{9,15},{10,... | collective-permute-start | bytes 1244168 | tf_op jit(solution)/shard_map/ppermute | solution.py:44
  88.3 39.4 %collective-permute-start.4 = (bf16[288,720]{1,0:T(8,128)(2,1)S(1)}, bf16[288,720]{1,0:T(8,128)(2,1)S(1)}, u32[]{:S(2)}, u32[]{:S(2)}) collective-permute-start(bf16[288,720]{1,0:T(8,128)(2,1)S(1)} %concatenate.142), channel_id=1, source_target_pairs={{0,4},{1,5},{2,6},{3,7},{4,0},{5,1},{6,2},{7,3},{8,12},{9,13},{10,... | collective-permute-start | bytes 1244168 | tf_op jit(solution)/shard_map/ppermute | solution.py:44
  89.4 40.7 %collective-permute-start.3 = (bf16[288,720]{1,0:T(8,128)(2,1)S(1)}, bf16[288,720]{1,0:T(8,128)(2,1)S(1)}, u32[]{:S(2)}, u32[]{:S(2)}) collective-permute-start(bf16[288,720]{1,0:T(8,128)(2,1)S(1)} %concatenate.142), channel_id=1, source_target_pairs={{0,2},{1,3},{2,0},{3,1},{4,6},{5,7},{6,4},{7,5},{8,10},{9,11},{10,... | collective-permute-start | bytes 1244168 | tf_op jit(solution)/shard_map/ppermute | solution.py:44
  100.5 37.1 %collective-permute-start.12 = (bf16[288,1728]{1,0:T(8,128)(2,1)}, bf16[288,1728]{1,0:T(8,128)(2,1)}, u32[]{:S(2)}, u32[]{:S(2)}) collective-permute-start(bf16[288,1728]{1,0:T(8,128)(2,1)} %concatenate.146), channel_id=1, source_target_pairs={{0,8},{8,0},{16,24},{24,16},{1,9},{9,1},{17,25},{25,17},{2,10},{10... | collective-permute-start | bytes 2985992 | tf_op jit(solution)/shard_map/ppermute | solution.py:40
  100.5 41.6 %collective-permute-start.13 = (bf16[288,1728]{1,0:T(8,128)(2,1)}, bf16[288,1728]{1,0:T(8,128)(2,1)}, u32[]{:S(2)}, u32[]{:S(2)}) collective-permute-start(bf16[288,1728]{1,0:T(8,128)(2,1)} %collective-permute-done.11), channel_id=1, source_target_pairs={{0,8},{8,0},{16,24},{24,16},{1,9},{9,1},{17,25},{25,17},{2,10},{10... | collective-permute-start | bytes 2985992 | tf_op jit(solution)/shard_map/ppermute | solution.py:40
  136.1 46.8 %collective-permute-start.6 = (bf16[288,2880]{1,0:T(8,128)(2,1)}, bf16[288,2880]{1,0:T(8,128)(2,1)}, u32[]{:S(2)}, u32[]{:S(2)}) collective-permute-start(bf16[288,2880]{1,0:T(8,128)(2,1)} %concatenate.144), channel_id=1, source_target_pairs={{0,16},{8,24},{16,0},{24,8},{1,17},{9,25},{17,1},{25,9},{2,18},{10... | collective-permute-start | bytes 4976648 | tf_op jit(solution)/shard_map/ppermute | solution.py:40
  148.2 34.9 %collective-permute-start.15 = (bf16[1152,512]{1,0:T(8,128)(2,1)S(1)}, bf16[1152,512]{1,0:T(8,128)(2,1)}, u32[]{:S(2)}, u32[]{:S(2)}) collective-permute-start(bf16[1152,512]{1,0:T(8,128)(2,1)S(1)} %slice.756), channel_id=1, source_target_pairs={{0,8},{8,0},{16,24},{24,16},{1,9},{9,1},{17,25},{25,17},{2,10},{10... | collective-permute-start | bytes 3538952 | tf_op jit(solution)/shard_map/ppermute | solution.py:40
  176.5 113.4 %all-to-all-start.3 = ((bf16[8,144,256]{2,1,0:T(8,128)(2,1)}), bf16[8,144,256]{2,1,0:T(8,128)(2,1)}, u32[]{:S(2)}, u32[]{:S(2)}) async-start(bf16[8,144,256]{2,1,0:T(8,128)(2,1)} %bitcast.57), calls=%async_computation.3 | async-start | bytes 1179648 | tf_op jit(solution)/shard_map/all_to_all | solution.py:163
  181.2 43.1 %collective-permute-start.17 = (bf16[1152,120]{1,0:T(8,128)(2,1)S(1)}, bf16[1152,120]{1,0:T(8,128)(2,1)S(1)}, u32[]{:S(2)}, u32[]{:S(2)}) collective-permute-start(bf16[1152,120]{1,0:T(8,128)(2,1)S(1)} %bitcast.269), channel_id=1, source_target_pairs={{0,8},{8,0},{16,24},{24,16},{1,9},{9,1},{17,25},{25,17},{2,10},{10... | collective-permute-start | bytes 829448 | tf_op jit(solution)/shard_map/ppermute | solution.py:40
  233.4 35.5 %collective-permute-start.18 = (bf16[1152,256]{1,0:T(8,128)(2,1)S(1)}, bf16[1152,256]{1,0:T(8,128)(2,1)S(1)}, u32[]{:S(2)}, u32[]{:S(2)}) collective-permute-start(bf16[1152,256]{1,0:T(8,128)(2,1)S(1)} %fusion.119), channel_id=1, source_target_pairs={{0,1},{1,0},{2,3},{3,2},{4,5},{5,4},{6,7},{7,6},{8,9},{9,8},{10,11... | collective-permute-start | bytes 1769480 | tf_op jit(solution)/shard_map/ppermute | solution.py:44
  262.8 60.4 %collective-permute-start.29 = (bf16[288,2304]{1,0:T(8,128)(2,1)}, bf16[288,2304]{1,0:T(8,128)(2,1)}, u32[]{:S(2)}, u32[]{:S(2)}) collective-permute-start(bf16[288,2304]{1,0:T(8,128)(2,1)} %concatenate.155), channel_id=1, source_target_pairs={{0,16},{8,24},{16,0},{24,8},{1,17},{9,25},{17,1},{25,9},{2,18},{10... | collective-permute-start | bytes 3981320 | tf_op jit(solution)/shard_map/ppermute | solution.py:40
  277.9 45.8 %collective-permute-start.19 = (bf16[1152,256]{1,0:T(8,128)(2,1)S(1)}, bf16[1152,256]{1,0:T(8,128)(2,1)S(1)}, u32[]{:S(2)}, u32[]{:S(2)}) collective-permute-start(bf16[1152,256]{1,0:T(8,128)(2,1)S(1)} %slice.1138), channel_id=1, source_target_pairs={{0,1},{1,0},{2,3},{3,2},{4,5},{5,4},{6,7},{7,6},{8,9},{9,8},{10,11... | collective-permute-start | bytes 1769480 | tf_op jit(solution)/shard_map/ppermute | solution.py:44
  289.9 65.3 %collective-permute-start.30 = (bf16[288,2304]{1,0:T(8,128)(2,1)}, bf16[288,2304]{1,0:T(8,128)(2,1)}, u32[]{:S(2)}, u32[]{:S(2)}) collective-permute-start(bf16[288,2304]{1,0:T(8,128)(2,1)} %concatenate.155), channel_id=1, source_target_pairs={{0,8},{8,0},{16,24},{24,16},{1,9},{9,1},{17,25},{25,17},{2,10},{10... | collective-permute-start | bytes 3981320 | tf_op jit(solution)/shard_map/ppermute | solution.py:40
  323.1 47.8 %collective-permute-start.25 = (bf16[288,2304]{1,0:T(8,128)(2,1)}, bf16[288,2304]{1,0:T(8,128)(2,1)S(1)}, u32[]{:S(2)}, u32[]{:S(2)}) collective-permute-start(bf16[288,2304]{1,0:T(8,128)(2,1)} %concatenate.153), channel_id=1, source_target_pairs={{0,8},{8,0},{16,24},{24,16},{1,9},{9,1},{17,25},{25,17},{2,10},{10... | collective-permute-start | bytes 3981320 | tf_op jit(solution)/shard_map/ppermute | solution.py:40
  399.3 218.1 %collective-permute-start.75 = (bf16[576,2304]{1,0:T(8,128)(2,1)}, bf16[576,2304]{1,0:T(8,128)(2,1)}, u32[]{:S(2)}, u32[]{:S(2)}) collective-permute-start(bf16[576,2304]{1,0:T(8,128)(2,1)} %convolution_convert_fusion), channel_id=1, source_target_pairs={{0,8},{8,0},{16,24},{24,16},{1,9},{9,1},{17,25},{25,17},{2,10},{10... | collective-permute-start | bytes 7962632 | tf_op jit(solution)/shard_map/ppermute | solution.py:40
  436.2 62.8 %collective-permute-start.34 = (bf16[1152,256]{1,0:T(8,128)(2,1)}, bf16[1152,256]{1,0:T(8,128)(2,1)}, u32[]{:S(2)}, u32[]{:S(2)}) collective-permute-start(bf16[1152,256]{1,0:T(8,128)(2,1)} %pad_maximum_fusion.29), channel_id=1, source_target_pairs={{0,0},{1,1},{2,8},{3,9},{4,4},{5,5},{6,12},{7,13},{8,2},{9,3},{10,... | collective-permute-start | bytes 1769480 | tf_op jit(solution)/shard_map/ppermute | solution.py:143
  490.4 52.9 %collective-permute-start.40 = (bf16[1152,256]{1,0:T(8,128)(2,1)S(1)}, bf16[1152,256]{1,0:T(8,128)(2,1)}, u32[]{:S(2)}, u32[]{:S(2)}) collective-permute-start(bf16[1152,256]{1,0:T(8,128)(2,1)S(1)} %multiply_convert_fusion.3), channel_id=1, source_target_pairs={{0,1},{1,0},{2,3},{3,2},{4,5},{5,4},{6,7},{7,6},{8,9},{9,8},{10,11... | collective-permute-start | bytes 1769480 | tf_op jit(solution)/shard_map/ppermute | solution.py:44
  538.6 82.4 %collective-permute-start.70 = (bf16[576,2304]{1,0:T(8,128)(2,1)}, bf16[576,2304]{1,0:T(8,128)(2,1)}, u32[]{:S(2)}, u32[]{:S(2)}) collective-permute-start(bf16[576,2304]{1,0:T(8,128)(2,1)} %convolution_convert_fusion.1), channel_id=1, source_target_pairs={{0,8},{8,0},{16,24},{24,16},{1,9},{9,1},{17,25},{25,17},{2,10},{10... | collective-permute-start | bytes 7962632 | tf_op jit(solution)/shard_map/ppermute | solution.py:40
  538.7 76.6 %collective-permute-start.60 = (bf16[576,1152]{1,0:T(8,128)(2,1)}, bf16[576,1152]{1,0:T(8,128)(2,1)}, u32[]{:S(2)}, u32[]{:S(2)}) collective-permute-start(bf16[576,1152]{1,0:T(8,128)(2,1)} %convolution_convert_fusion.3), channel_id=1, source_target_pairs={{0,8},{8,0},{16,24},{24,16},{1,9},{9,1},{17,25},{25,17},{2,10},{10... | collective-permute-start | bytes 3981320 | tf_op jit(solution)/shard_map/ppermute | solution.py:40
  614.2 63.0 %collective-permute-start.41 = (bf16[1152,512]{1,0:T(8,128)(2,1)}, bf16[1152,512]{1,0:T(8,128)(2,1)}, u32[]{:S(2)}, u32[]{:S(2)}) collective-permute-start(bf16[1152,512]{1,0:T(8,128)(2,1)} %pad_maximum_fusion.19), channel_id=1, source_target_pairs={{0,8},{8,0},{16,24},{24,16},{1,9},{9,1},{17,25},{25,17},{2,10},{10... | collective-permute-start | bytes 3538952 | tf_op jit(solution)/shard_map/ppermute | solution.py:40
  652.2 39.1 %collective-permute-start.76 = (bf16[288,2304]{1,0:T(8,128)(2,1)}, bf16[288,2304]{1,0:T(8,128)(2,1)}, u32[]{:S(2)}, u32[]{:S(2)}) collective-permute-start(bf16[288,2304]{1,0:T(8,128)(2,1)} %fusion.24), channel_id=1, source_target_pairs={{0,16},{8,24},{16,0},{24,8},{1,17},{9,25},{17,1},{25,9},{2,18},{10... | collective-permute-start | bytes 3981320 | tf_op jit(solution)/shard_map/ppermute | solution.py:40
  664.5 47.4 %collective-permute-start.71 = (bf16[288,2304]{1,0:T(8,128)(2,1)}, bf16[288,2304]{1,0:T(8,128)(2,1)}, u32[]{:S(2)}, u32[]{:S(2)}) collective-permute-start(bf16[288,2304]{1,0:T(8,128)(2,1)} %fusion.23), channel_id=1, source_target_pairs={{0,16},{8,24},{16,0},{24,8},{1,17},{9,25},{17,1},{25,9},{2,18},{10... | collective-permute-start | bytes 3981320 | tf_op jit(solution)/shard_map/ppermute | solution.py:40
  691.0 62.1 %collective-permute-start.45 = (bf16[576,1728]{1,0:T(8,128)(2,1)}, bf16[576,1728]{1,0:T(8,128)(2,1)}, u32[]{:S(2)}, u32[]{:S(2)}) collective-permute-start(bf16[576,1728]{1,0:T(8,128)(2,1)} %convolution_convert_fusion.2), channel_id=1, source_target_pairs={{0,8},{8,0},{16,24},{24,16},{1,9},{9,1},{17,25},{25,17},{2,10},{10... | collective-permute-start | bytes 5971976 | tf_op jit(solution)/shard_map/ppermute | solution.py:40
  696.3 64.3 %collective-permute-start.77 = (bf16[288,576]{1,0:T(8,128)(2,1)}, bf16[288,576]{1,0:T(8,128)(2,1)}, u32[]{:S(2)}, u32[]{:S(2)}) collective-permute-start(bf16[288,576]{1,0:T(8,128)(2,1)} %get-tuple-element.180), channel_id=1, source_target_pairs={{0,2},{1,3},{2,0},{3,1},{4,6},{5,7},{6,4},{7,5},{8,10},{9,11},{10,... | collective-permute-start | bytes 995336 | tf_op jit(solution)/shard_map/ppermute | solution.py:44
  696.3 64.3 %collective-permute-start.79 = (bf16[288,576]{1,0:T(8,128)(2,1)}, bf16[288,576]{1,0:T(8,128)(2,1)}, u32[]{:S(2)}, u32[]{:S(2)}) collective-permute-start(bf16[288,576]{1,0:T(8,128)(2,1)} %get-tuple-element.181), channel_id=1, source_target_pairs={{0,6},{1,7},{2,4},{3,5},{4,2},{5,3},{6,0},{7,1},{8,14},{9,15},{10,... | collective-permute-start | bytes 995336 | tf_op jit(solution)/shard_map/ppermute | solution.py:44
  711.9 51.2 %collective-permute-start.78 = (bf16[288,576]{1,0:T(8,128)(2,1)}, bf16[288,576]{1,0:T(8,128)(2,1)}, u32[]{:S(2)}, u32[]{:S(2)}) collective-permute-start(bf16[288,576]{1,0:T(8,128)(2,1)} %get-tuple-element.182), channel_id=1, source_target_pairs={{0,4},{1,5},{2,6},{3,7},{4,0},{5,1},{6,2},{7,3},{8,12},{9,13},{10,... | collective-permute-start | bytes 995336 | tf_op jit(solution)/shard_map/ppermute | solution.py:44
  746.2 56.9 %all-to-all-start.4 = ((bf16[8,144,256]{2,1,0:T(8,128)(2,1)}), bf16[8,144,256]{2,1,0:T(8,128)(2,1)}, u32[]{:S(2)}, u32[]{:S(2)}) async-start(bf16[8,144,256]{2,1,0:T(8,128)(2,1)} %bitcast.75), calls=%async_computation.4 | async-start | bytes 1179648 | tf_op jit(solution)/shard_map/all_to_all | solution.py:168
  760.6 40.2 %collective-permute-start.73 = (bf16[288,576]{1,0:T(8,128)(2,1)}, bf16[288,576]{1,0:T(8,128)(2,1)S(1)}, u32[]{:S(2)}, u32[]{:S(2)}) collective-permute-start(bf16[288,576]{1,0:T(8,128)(2,1)} %get-tuple-element.185), channel_id=1, source_target_pairs={{0,4},{1,5},{2,6},{3,7},{4,0},{5,1},{6,2},{7,3},{8,12},{9,13},{10,... | collective-permute-start | bytes 995336 | tf_op jit(solution)/shard_map/ppermute | solution.py:44
  760.6 45.0 %collective-permute-start.46 = (bf16[288,1728]{1,0:T(8,128)(2,1)}, bf16[288,1728]{1,0:T(8,128)(2,1)}, u32[]{:S(2)}, u32[]{:S(2)}) collective-permute-start(bf16[288,1728]{1,0:T(8,128)(2,1)} %fusion.28), channel_id=1, source_target_pairs={{0,16},{8,24},{16,0},{24,8},{1,17},{9,25},{17,1},{25,9},{2,18},{10... | collective-permute-start | bytes 2985992 | tf_op jit(solution)/shard_map/ppermute | solution.py:40
  (217 other events, 3164.7 us)

commit v2 on v1

--- a/solution.py
+++ b/solution.py
@@ -1,6 +1,10 @@
+import functools
+
 import jax
 import jax.numpy as jnp
 from jax import lax
+from jax.experimental import pallas as pl
+from jax.experimental.pallas import tpu as pltpu
 from jax.sharding import PartitionSpec as P
 
 D = 1152
@@ -11,6 +15,7 @@
 MASK_FILL = -1e30
 BF = jnp.bfloat16
 F32 = jnp.float32
+LOG_SCALE = HD ** -0.5 * 1.4426950408889634
 
 
 def dot_nn(a, b):
@@ -60,33 +65,78 @@
     return back, jnp.sum(grad, axis=1), jnp.sum(grad * normed, axis=1)
 
 
-def attend_forward(q_t, k_t, v_t, valid):
-    heads = q_t.shape[0] // HD
-    q3, k3, v3 = (a.reshape(heads, HD, a.shape[1]) for a in (q_t, k_t, v_t))
-    s = jnp.einsum("hdk,hdq->hkq", k3, q3, preferred_element_type=F32) * HD ** -0.5
-    if valid is not None:
-        s = jnp.where(valid[None, :, None], s, MASK_FILL)
-    top = jnp.max(s, axis=1, keepdims=True)
-    lse = top + jnp.log(jnp.sum(jnp.exp(s - top), axis=1, keepdims=True))
-    p = jnp.exp(s - lse).astype(BF)
-    out = jnp.einsum("hdk,hkq->hdq", v3, p, preferred_element_type=F32)
-    return out.reshape(q_t.shape).astype(BF), lse
-
-
-def attend_backward(q_t, k_t, v_t, valid, lse, do_t):
-    heads = q_t.shape[0] // HD
-    q3, k3, v3, do3 = (a.reshape(heads, HD, a.shape[1]) for a in (q_t, k_t, v_t, do_t))
-    s = jnp.einsum("hdk,hdq->hkq", k3, q3, preferred_element_type=F32) * HD ** -0.5
-    if valid is not None:
-        s = jnp.where(valid[None, :, None], s, MASK_FILL)
-    p = jnp.exp(s - lse)
-    dv = jnp.einsum("hdq,hkq->hdk", do3, p.astype(BF), preferred_element_type=F32)
-    dp = jnp.einsum("hdk,hdq->hkq", v3, do3, preferred_element_type=F32)
-    ds = p * (dp - jnp.sum(dp * p, axis=1, keepdims=True))
-    ds = (ds * HD ** -0.5).astype(BF)
-    dq = jnp.einsum("hdk,hkq->hdq", k3, ds, preferred_element_type=F32)
-    dk = jnp.einsum("hdq,hkq->hdk", q3, ds, preferred_element_type=F32)
-    return dq.reshape(q_t.shape).astype(BF), dk.reshape(k_t.shape).astype(BF), dv.reshape(k_t.shape).astype(BF)
+def dot_at(a, b, a_dim, b_dim):
+    return lax.dot_general(a, b, (((a_dim,), (b_dim,)), ((), ())), preferred_element_type=F32)
+
+
+def masked_scores(scores, len_ref):
+    if len_ref is None:
+        return scores
+    return jnp.where(lax.broadcasted_iota(jnp.int32, scores.shape, 1) < len_ref[0], scores, MASK_FILL)
+
+
+def forward_kernel(*refs):
+    len_ref = refs[0] if len(refs) == 6 else None
+    q_ref, k_ref, v_ref, out_ref, lse_ref = refs[-5:]
+    for h in range(q_ref.shape[0] // HD):
+        head = slice(HD * h, HD * h + HD)
+        scores = masked_scores(dot_at(q_ref[head, :], k_ref[head, :], 0, 0), len_ref)
+        top = jnp.max(scores, axis=1, keepdims=True)
+        probs = jnp.exp2((scores - top) * LOG_SCALE)
+        total = jnp.sum(probs, axis=1, keepdims=True)
+        out = dot_at(probs.astype(BF), v_ref[head, :], 1, 1) / total
+        out_ref[head, :] = out.T.astype(BF)
+        lse_ref[0, :, h : h + 1] = top * LOG_SCALE + jnp.log2(total)
+
+
+def backward_kernel(*refs):
+    len_ref = refs[0] if len(refs) == 9 else None
+    q_ref, k_ref, v_ref, lse_ref, do_ref, dq_ref, dk_ref, dv_ref = refs[-8:]
+    for h in range(q_ref.shape[0] // HD):
+        head = slice(HD * h, HD * h + HD)
+        q, k, v, do = q_ref[head, :], k_ref[head, :], v_ref[head, :], do_ref[head, :]
+        scores = masked_scores(dot_at(q, k, 0, 0), len_ref)
+        probs = jnp.exp2(scores * LOG_SCALE - lse_ref[0, :, h : h + 1])
+        dv_ref[head, :] = dot_at(do, probs.astype(BF), 1, 0).astype(BF)
+        dp = dot_at(do, v, 0, 0)
+        ds = probs * (dp - jnp.sum(dp * probs, axis=1, keepdims=True)) * HD ** -0.5
+        ds = ds.astype(BF)
+        dq_ref[head, :] = dot_at(ds, k, 1, 1).T.astype(BF)
+        dk_ref[head, :] = dot_at(q, ds, 1, 0).astype(BF)
+
+
+def attend_call(kernel, args, length, outs, group):
+    def spec(a):
+        if len(a.shape) == 3:
+            return pl.BlockSpec((1,) + a.shape[1:], lambda i: (i, 0, 0))
+        return pl.BlockSpec((group, a.shape[1]), lambda i: (i, 0))
+
+    specs = [spec(a) for a in args]
+    if length is not None:
+        specs, args = [pl.BlockSpec(memory_space=pltpu.SMEM)] + specs, [length] + args
+    return pl.pallas_call(
+        kernel,
+        grid=(outs[0].shape[0] // group,),
+        in_specs=specs,
+        out_specs=[spec(o) for o in outs],
+        out_shape=outs,
+        compiler_params=pltpu.CompilerParams(vmem_limit_bytes=50 * 2**20),
+    )(*args)
+
+
+def attend_forward(q_t, k_t, v_t, length):
+    group = HD * (2 if q_t.shape[0] % (2 * HD) == 0 else 1)
+    outs = [
+        jax.ShapeDtypeStruct(q_t.shape, BF),
+        jax.ShapeDtypeStruct((q_t.shape[0] // group, q_t.shape[1], group // HD), F32),
+    ]
+    return attend_call(forward_kernel, [q_t, k_t, v_t], length, outs, group)
+
+
+def attend_backward(q_t, k_t, v_t, length, lse, do_t):
+    group = HD * lse.shape[2]
+    outs = [jax.ShapeDtypeStruct(a.shape, BF) for a in (q_t, k_t, v_t)]
+    return attend_call(backward_kernel, [q_t, k_t, v_t, lse, do_t], length, outs, group)
 
 
 def shards(
@@ -127,7 +177,6 @@
     steps = time_table.shape[2]
     ups = up_bias.shape[0]
     core, low_z, micro = r & 1, (c >> 1) & 1, c // half
-    home_row = (r - core) | low_z
     at_home = core == low_z
     r_rev = bit_reverse(r, row_bits)
 
@@ -248,9 +297,6 @@
     up_w, _, gate_three = gather_weights([up_weight], gate_two)
     down_w, _, _ = gather_weights([down_weight.T], gate_three)
 
-    lengths_steps = lax.all_gather(jnp.stack([text_length[:, 0], time_index[:, 0]]), "row")
-    length = lengths_steps[home_row, 0, micro]
-    step_all = lengths_steps[:, 1, :].T.reshape(2 * rows)
     step_ids = jnp.arange(steps, dtype=jnp.int32)
     onehot = (time_index[:, 0][:, None] == step_ids[None, :]).astype(F32)
     modulation = lax.dot_general(
@@ -260,42 +306,48 @@
         precision=lax.Precision.HIGHEST,
         preferred_element_type=F32,
     ).reshape(2, 6, feat) + shift_table[None]
-    small = jnp.concatenate(
+    same = [
+        jnp.broadcast_to(b.reshape(1, -1, feat), (2, b.shape[0] // feat, feat))
+        for b in (out_bias, cross_out_bias, down_bias, query_bias, value_bias, cross_query_bias, cross_value_bias, up_bias)
+    ]
+    lengths = jnp.broadcast_to(text_length.astype(F32)[:, :, None], (2, 1, feat))
+    small = jnp.concatenate([modulation, lengths] + same, axis=1).transpose(0, 2, 1)
+    small_high = lax.reduce_precision(small, 8, 7)
+    small_rest = small - small_high
+    small_mid = lax.reduce_precision(small_rest, 8, 7)
+    small_low = small_rest - small_mid
+    extra = jnp.concatenate(
+        [text_tokens.transpose(0, 2, 1)] + [p.astype(BF) for p in (small_high, small_mid, small_low)], axis=2
+    )
+    blocks = block_input.reshape(2, feat, half, width).transpose(0, 2, 1, 3).reshape(cols, feat, width)
+    blocks = jnp.concatenate([blocks, jnp.repeat(extra, half, axis=0)], axis=2)
+    blocks = lax.all_to_all(blocks, "col", 0, 0, tiled=True).reshape(D, -1)
+    arrived = place_swap(blocks)
+    arrived_local = to_local(arrived)
+    small_n = small.shape[2]
+
+    def small_of(value):
+        parts = [value[:, width + texts + i * small_n : width + texts + (i + 1) * small_n].astype(F32) for i in range(3)]
+        return parts[0] + parts[1] + parts[2]
+
+    model_rows = small_of(arrived_local)
+    shift_a, scale_a, gate_a, shift_m, scale_m, gate_m, length_row, out_b, cout_b, down_b = (
+        model_rows[:, i : i + 1] for i in range(10)
+    )
+    length = length_row[0].astype(jnp.int32)
+    col_rows = small_of(arrived).reshape(cols, feat, small_n)
+    col_rows = jnp.concatenate(
         [
-            modulation.reshape(12, feat),
-            out_bias[None],
-            cross_out_bias[None],
-            down_bias[None],
-            query_bias[None],
-            value_bias[None],
-            cross_query_bias[None],
-            cross_value_bias[None],
-            up_bias.reshape(ups // feat, feat),
+            lax.dynamic_index_in_dim(col_rows, c ^ (e << 1), 0, keepdims=False)[:, 10:].T.reshape(-1, 1, feat)
+            for e in range(half)
         ],
-        axis=0,
-    )
-    small = lax.all_gather(small, "col")
-    mods = small[:, :12].transpose(1, 0, 2).reshape(2, 6, D)
-    mods = lax.dynamic_index_in_dim(mods, micro, 0, keepdims=False)
-    mods = jnp.where(at_home, mods, row_swap(mods, rows, 1))
-    model_rows = jnp.concatenate([mods, small[:, 12:15].transpose(1, 0, 2).reshape(3, D)], axis=0)
-    model_rows = to_local(model_rows.T)
-    shift_a, scale_a, gate_a, shift_m, scale_m, gate_m, out_b, cout_b, down_b = (
-        model_rows[:, i : i + 1] for i in range(9)
-    )
-    col_rows = [
-        lax.dynamic_index_in_dim(small, c ^ (e << 1), 0, keepdims=False)[15:] for e in range(half)
-    ]
-    col_rows = jnp.stack(col_rows, axis=1)
+        axis=1,
+    )
     q_b, v_b, cq_b, cv_b = (col_rows[i].reshape(half * feat, 1) for i in range(4))
     up_b = col_rows[4:].transpose(1, 0, 2).reshape(half * ups, 1)
-
-    text_blocks = text_tokens.transpose(0, 2, 1)
-    text_t = lax.all_to_all(jnp.repeat(text_blocks, half, axis=0), "col", 0, 0, tiled=True).reshape(D, texts)
-    text_t = to_local(jnp.where(at_home, text_t, row_swap(text_t, rows, 1)))
-    valid = jnp.arange(texts, dtype=jnp.int32) < length
-
-    resid = tokens_in(block_input).astype(F32)
+    text_t = arrived_local[:, width : width + texts]
+
+    resid = arrived_local[:, :width].astype(F32)
     cot = tokens_in(out_grad).astype(F32)
     normed_a, inv_a = layer_norm(resid)
     attn_full = gather_pair((normed_a * (1.0 + scale_a) + shift_a).astype(BF))
@@ -312,7 +364,7 @@
     cq_t = (dot_tn(cq_w, cross_full) + cq_b).astype(BF)
     ck_t = dot_tn(ck_w, text_t).astype(BF)
     cv_t = (dot_tn(cv_w, text_t) + cv_b).astype(BF)
-    catt, clse = attend_forward(cq_t, ck_t, cv_t, valid)
+    catt, clse = attend_forward(cq_t, ck_t, cv_t, length)
     after_cross = after_attn + reduce_pair(dot_nn(cout_w, catt)) + cout_b
     normed_m, inv_m = layer_norm(after_cross)
     mlp_full = gather_pair((normed_m * (1.0 + scale_m) + shift_m).astype(BF))
@@ -336,7 +388,7 @@
     g_cout_b = jnp.sum(grad_cross, axis=1)
     low_cross = gather_pair(grad_cross.astype(BF))
     dcatt = dot_tn(cout_w, low_cross).astype(BF)
-    dcq, dck, dcv = attend_backward(cq_t, ck_t, cv_t, valid, clse, dcatt)
+    dcq, dck, dcv = attend_backward(cq_t, ck_t, cv_t, length, clse, dcatt)
     g_cq_b = jnp.sum(dcq.astype(F32), axis=1)
     g_cv_b = jnp.sum(dcv.astype(F32), axis=1)
     grad_res = grad_cross + reduce_pair(dot_nn(cq_w, dcq))
@@ -383,10 +435,12 @@
     small_g = lax.all_to_all(small_g, "col", 0, 0, tiled=True)
     mod_g = small_g[:, :6].reshape(2, cols // 8, 2, 2, 6, feat).sum(axis=(1, 3))
     bias_g = small_g[:, 6:].sum(axis=0)
-    small_g = lax.all_gather(jnp.concatenate([mod_g.reshape(24, feat), bias_g], axis=0), "row")
+    step_rows = jnp.broadcast_to(time_index.astype(F32), (2, feat))
+    small_g = lax.all_gather(jnp.concatenate([mod_g.reshape(24, feat), bias_g, step_rows], axis=0), "row")
+    step_all = small_g[:, -2:, 0].T.reshape(2 * rows).astype(jnp.int32)
     mod_g = small_g[:, :24].reshape(rows // 2, 2, 2, 2, 6, feat).sum(axis=1)
     mod_g = mod_g.transpose(1, 0, 2, 3, 4).reshape(2 * rows, 6, feat)
-    bias_g = small_g[:, 24:].sum(axis=0)
+    bias_g = small_g[:, 24:-2].sum(axis=0)
     g_shift = mod_g.sum(axis=0)
     onehot_all = (step_all[:, None] == step_ids[None, :]).astype(F32)
     g_time = lax.dot_general(

time: 853 us -> 797 us (0.934)
  matrix products: 210 us -> 129 us
  blocking collectives: 68.1 us -> 5.49 us
  starting transfers between devices: 138 us -> 173 us
  Pallas kernels: 0 us -> 32 us
  waiting for transfers between devices: 266 us -> 295 us
    dot_general x12 -> x0, matrix products: 90.5 us -> none  [the longest x2 26.6 us: attend_backward(): dq = jnp.einsum('hdk,hkq->hdq', k3, ds, preferred_element_type=F32)]
    all_gather x3 -> x1, blocking collectives: 68.1 us -> 5.49 us  [shards(): lax.all_gather(jnp.concatenate([mod_g.reshape(24, feat), bias_g, step_row...]
    pallas_call x0 -> x4, Pallas kernels: none -> 32 us  [attend_call(): pl.pallas_call(kernel, grid=(outs[0].shape[0] // group,), in_specs=specs,...]
    ppermute x45, starting transfers between devices: 63.4 us -> 93.6 us  [col_swap(): return lax.ppermute(value, 'col', [(i, i ^ mask) for i in range(cols)])]
    ppermute x31 -> x29, waiting for transfers between devices: 55.8 us -> 80.5 us  [row_swap(): return lax.ppermute(value, 'row', [(i, i ^ bit) for i in range(rows)])]
    ppermute x45, waiting for transfers between devices: 191 us -> 211 us  [col_swap(): return lax.ppermute(value, 'col', [(i, i ^ mask) for i in range(cols)])]
    all_to_all x2, waiting for transfers between devices: 12 us -> 0.01 us  [tokens_out(): blocks = lax.all_to_all(blocks, 'col', 0, 0, tiled=True)]
    concatenate x4, local copies, waits for them, and re-layouts: 24.8 us -> 14.7 us  [gather_weights(): parts = [jnp.concatenate(pieces, axis=1)]]
  transfers between devices with their start and end apart: 87 -> 84, of which waited for: 30 -> 30; matrix products, arithmetic and copies ran while one was open for 38% -> 29% of each run, Pallas kernels for 0% -> 3%
where the time goes in v2:
time: 797 us; the launch traced here: 785 us
  waiting for transfers between devices  295 us (37%)
  starting transfers between devices  173 us (22%)
  matrix products  129 us (16%)
  local copies, waits for them, and re-layouts  87.5 us (11%)
  other arithmetic  59.6 us (7%)
  Pallas kernels  32 us (4%)
    ppermute x45, waiting for transfers between devices, col_swap(): return lax.ppermute(value, 'col', [(i, i ^ mask) for i in range(cols)])  211 us
    ppermute x45, starting transfers between devices, col_swap(): return lax.ppermute(value, 'col', [(i, i ^ mask) for i in range(cols)])  93.6 us
    ppermute x29, waiting for transfers between devices, row_swap(): return lax.ppermute(value, 'row', [(i, i ^ bit) for i in range(rows)])  80.5 us
    dot_general x21, matrix products, dot_nt(): lax.dot_general(a, b, (((1,), (1,)), ((), ())), preferred_element_type=F32)  60.2 us
    dot_general x8, matrix products, dot_tn(): lax.dot_general(a, b, (((0,), (0,)), ((), ())), preferred_element_type=F32)  32.6 us
    pallas_call x4, Pallas kernels, attend_call(): pl.pallas_call(kernel, grid=(outs[0].shape[0] // group,), in_specs=specs,...  32 us
    dot_general x8, matrix products, dot_nn(): lax.dot_general(a, b, (((1,), (0,)), ((), ())), preferred_element_type=F32)  29.9 us
    unnamed x308, local copies, waits for them, and re-layouts  25.6 us
  transfers between devices with their start and end apart: 84, of which 30 were waited for; matrix products, arithmetic and copies ran while one was open for 29% of the time, Pallas kernels for 3%

profile of v2, /device:TPU:0, one launch (start us, length us, event | category | flops | bytes accessed | tf_op | source)
XLA Modules:
  0.0 784.9 jit_solution(13705792523025804447)
XLA Ops:
  21.5 5.8 collective-permute-start.3
  38.8 27.6 %collective-permute-done.3 = bf16[288,720]{1,0:T(8,128)(2,1)S(1)} collective-permute-done((bf16[288,720]{1,0:T(8,128)(2,1)S(1)}, bf16[288,720]{1,0:T(8,128)(2,1)S(1)}, u32[]{:S(2)}, u32[]{:S(2)}) %collective-permute-start.3) | collective-permute-done | bytes 414752 | tf_op jit(solution)/shard_map/ppermute | solution.py:49
  67.5 19.0 %collective-permute-done.2 = bf16[288,720]{1,0:T(8,128)(2,1)S(1)} collective-permute-done((bf16[288,720]{1,0:T(8,128)(2,1)S(1)}, bf16[288,720]{1,0:T(8,128)(2,1)S(1)}, u32[]{:S(2)}, u32[]{:S(2)}) %collective-permute-start.2) | collective-permute-done | bytes 414752 | tf_op jit(solution)/shard_map/ppermute | solution.py:49
  105.6 9.5 %collective-permute-start = (bf16[1152,430]{0,1:T(8,128)(2,1)}, bf16[1152,430]{0,1:T(8,128)(2,1)}, u32[]{:S(2)}, u32[]{:S(2)}) collective-permute-start(bf16[1152,430]{0,1:T(8,128)(2,1)} %copy.207), channel_id=1, source_target_pairs={{0,0},{1,1},{2,8},{3,9},{4,4},{5,5},{6,12},{7,13},{8,2},{9,3},{10,... | collective-permute-start | bytes 2972168 | tf_op jit(solution)/shard_map/ppermute | solution.py:192
  115.1 8.7 %collective-permute-start.11 = (bf16[288,1728]{1,0:T(8,128)(2,1)}, bf16[288,1728]{1,0:T(8,128)(2,1)}, u32[]{:S(2)}, u32[]{:S(2)}) collective-permute-start(bf16[288,1728]{1,0:T(8,128)(2,1)} %concatenate.146), channel_id=1, source_target_pairs={{0,8},{8,0},{16,24},{24,16},{1,9},{9,1},{17,25},{25,17},{2,10},{10... | collective-permute-start | bytes 2985992 | tf_op jit(solution)/shard_map/ppermute | solution.py:45
  123.9 28.3 %collective-permute-done.10 = bf16[288,1728]{1,0:T(8,128)(2,1)} collective-permute-done((bf16[288,1728]{1,0:T(8,128)(2,1)}, bf16[288,1728]{1,0:T(8,128)(2,1)}, u32[]{:S(2)}, u32[]{:S(2)}) %collective-permute-start.10) | collective-permute-done | bytes 995360 | tf_op jit(solution)/shard_map/ppermute | solution.py:45
  166.0 12.8 %collective-permute-done.13 = bf16[1152,256]{1,0:T(8,128)(2,1)S(1)} collective-permute-done((bf16[1152,256]{1,0:T(8,128)(2,1)}, bf16[1152,256]{1,0:T(8,128)(2,1)S(1)}, u32[]{:S(2)}, u32[]{:S(2)}) %collective-permute-start.13) | collective-permute-done | bytes 589856 | tf_op jit(solution)/shard_map/ppermute | solution.py:49
  189.9 9.5 %shard_map.416 = (bf16[576,512]{1,0:T(8,128)(2,1)S(1)}, f32[4,512,2]{2,1,0:T(8,128)S(1)}) custom-call(bf16[576,512]{1,0:T(8,128)(2,1)S(1)} %slice.807.refs_0_, bf16[576,1024]{1,0:T(8,128)(2,1)S(1)} %get-tuple-element.244.refs_1_, bf16[576,1024]{1,0:T(8,128)(2,1)} %get-tuple-element.243.refs_2_), custom_call_target="tpu_custom_call" | custom-call | tf_op jit(solution)/shard_map/pallas_call | solution.py:117
  202.3 16.5 %collective-permute-start.26 = (bf16[288,576]{1,0:T(8,128)(2,1)}, bf16[288,576]{1,0:T(8,128)(2,1)}, u32[]{:S(2)}, u32[]{:S(2)}) collective-permute-start(bf16[288,576]{1,0:T(8,128)(2,1)} %param.45), channel_id=1, source_target_pairs={{0,4},{1,5},{2,6},{3,7},{4,0},{5,1},{6,2},{7,3},{8,12},{9,13},{10,... | collective-permute-start | bytes 995336 | tf_op jit(solution)/shard_map/ppermute | solution.py:49
  223.9 14.5 %all-to-all-start.2 = ((bf16[8,144,256]{2,1,0:T(8,128)(2,1)}), bf16[8,144,256]{2,1,0:T(8,128)(2,1)}, u32[]{:S(2)}, u32[]{:S(2)}) async-start(bf16[8,144,256]{2,1,0:T(8,128)(2,1)} %bitcast.194), calls=%async_computation.2 | async-start | bytes 1179648 | tf_op jit(solution)/shard_map/all_to_all | solution.py:212
  238.4 8.6 %collective-permute-done.18 = bf16[288,576]{1,0:T(8,128)(2,1)} collective-permute-done((bf16[288,576]{1,0:T(8,128)(2,1)}, bf16[288,576]{1,0:T(8,128)(2,1)}, u32[]{:S(2)}, u32[]{:S(2)}) %collective-permute-start.18) | collective-permute-done | bytes 331808 | tf_op jit(solution)/shard_map/ppermute | solution.py:49
  270.9 12.3 %collective-permute-start.20 = (bf16[288,576]{1,0:T(8,128)(2,1)}, bf16[288,576]{1,0:T(8,128)(2,1)S(1)}, u32[]{:S(2)}, u32[]{:S(2)}) collective-permute-start(bf16[288,576]{1,0:T(8,128)(2,1)} %bitcast.24), channel_id=1, source_target_pairs={{0,4},{1,5},{2,6},{3,7},{4,0},{5,1},{6,2},{7,3},{8,12},{9,13},{10,... | collective-permute-start | bytes 995336 | tf_op jit(solution)/shard_map/ppermute | solution.py:49
  283.3 22.9 %collective-permute-done.20 = bf16[288,576]{1,0:T(8,128)(2,1)S(1)} collective-permute-done((bf16[288,576]{1,0:T(8,128)(2,1)}, bf16[288,576]{1,0:T(8,128)(2,1)S(1)}, u32[]{:S(2)}, u32[]{:S(2)}) %collective-permute-start.20) | collective-permute-done | bytes 331808 | tf_op jit(solution)/shard_map/ppermute | solution.py:49
  307.0 6.1 collective-permute-start.33
  324.1 24.5 %collective-permute-done.22 = bf16[288,2304]{1,0:T(8,128)(2,1)} collective-permute-done((bf16[288,2304]{1,0:T(8,128)(2,1)}, bf16[288,2304]{1,0:T(8,128)(2,1)}, u32[]{:S(2)}, u32[]{:S(2)}) %collective-permute-start.22) | collective-permute-done | bytes 1327136 | tf_op jit(solution)/shard_map/ppermute | solution.py:45
  351.4 6.8 multiply_convert_fusion
  358.2 7.7 collective-permute-done.34
  365.8 7.9 %convert_reduce_fusion = (f32[2304]{0:T(1024)S(1)}, bf16[2304,512]{0,1:T(8,128)(2,1)S(1)}) fusion(f32[2304,512]{0,1:T(8,128)S(1)} %get-tuple-element.373, bf16[1152,256]{1,0:T(8,128)(2,1)S(1)} %collective-permute-done.34, bf16[1152,256]{1,0:T(8,128)(2,1)S(1)} %copy-done.44, bf16[288,2304]{1,0:T(8,128)(2,1)} %collective-permute-done.24, ...), kind=kOutput, calls=%fused_computation.13 | convolution fusion | flops 2767451904 | bytes 13575168 | tf_op jit(solution)/shard_map/dot_general | solution.py:26
  373.8 7.1 fusion.71
  381.8 5.9 fusion.72
  397.8 8.1 %collective-permute-done.31 = bf16[1152,256]{1,0:T(8,128)(2,1)} collective-permute-done((bf16[1152,256]{1,0:T(8,128)(2,1)}, bf16[1152,256]{1,0:T(8,128)(2,1)}, u32[]{:S(2)}, u32[]{:S(2)}) %collective-permute-start.31) | collective-permute-done | bytes 589856 | tf_op jit(solution)/shard_map/ppermute | solution.py:49
  405.9 11.3 %collective-permute-done.35 = bf16[1152,256]{1,0:T(8,128)(2,1)} collective-permute-done((bf16[1152,256]{1,0:T(8,128)(2,1)}, bf16[1152,256]{1,0:T(8,128)(2,1)}, u32[]{:S(2)}, u32[]{:S(2)}) %collective-permute-start.35) | collective-permute-done | bytes 589856 | tf_op jit(solution)/shard_map/ppermute | solution.py:49
  435.9 6.1 collective-permute-start.32
  519.9 5.8 collective-permute-start.55
  535.4 6.1 collective-permute-done.56
  545.9 14.2 %shard_map.419 = (bf16[576,512]{1,0:T(8,128)(2,1)S(1)}, bf16[576,1024]{1,0:T(8,128)(2,1)S(1)}, bf16[576,1024]{1,0:T(8,128)(2,1)}) custom-call(bf16[576,512]{1,0:T(8,128)(2,1)S(1)} %slice.807.refs_0_, bf16[576,1024]{1,0:T(8,128)(2,1)} %copy-done.2, bf16[576,1024]{1,0:T(8,128)(2,1)} %get-tuple-element.243.refs_2_, f32[4,512,2]{2,1,0:T(8,128)S(1)} %copy-done.6, ...), custom_call_target="tpu_custom_call" | custom-call | tf_op jit(solution)/shard_map/pallas_call | solution.py:117
  577.5 7.4 collective-permute-done.59
  590.7 11.1 %collective-permute-done.61 = bf16[288,288]{1,0:T(8,128)(2,1)S(1)} collective-permute-done((bf16[288,288]{1,0:T(8,128)(2,1)S(1)}, bf16[288,288]{1,0:T(8,128)(2,1)S(1)}, u32[]{:S(2)}, u32[]{:S(2)}) %collective-permute-start.61) | collective-permute-done | bytes 165920 | tf_op jit(solution)/shard_map/ppermute | solution.py:49
  647.5 14.0 %collective-permute-done.69 = bf16[288,2304]{1,0:T(8,128)(2,1)} collective-permute-done((bf16[288,2304]{1,0:T(8,128)(2,1)}, bf16[288,2304]{1,0:T(8,128)(2,1)}, u32[]{:S(2)}, u32[]{:S(2)}) %collective-permute-start.69) | collective-permute-done | bytes 1327136 | tf_op jit(solution)/shard_map/ppermute | solution.py:45
  714.1 12.1 %collective-permute-done.72 = bf16[288,576]{1,0:T(8,128)(2,1)} collective-permute-done((bf16[288,576]{1,0:T(8,128)(2,1)}, bf16[288,576]{1,0:T(8,128)(2,1)}, u32[]{:S(2)}, u32[]{:S(2)}) %collective-permute-start.72) | collective-permute-done | bytes 331808 | tf_op jit(solution)/shard_map/ppermute | solution.py:49
  726.3 22.5 %collective-permute-done.71 = bf16[288,576]{1,0:T(8,128)(2,1)S(1)} collective-permute-done((bf16[288,576]{1,0:T(8,128)(2,1)}, bf16[288,576]{1,0:T(8,128)(2,1)S(1)}, u32[]{:S(2)}, u32[]{:S(2)}) %collective-permute-start.71) | collective-permute-done | bytes 331808 | tf_op jit(solution)/shard_map/ppermute | solution.py:49
  759.6 16.5 %collective-permute-done.46 = bf16[288,432]{1,0:T(8,128)(2,1)S(1)} collective-permute-done((bf16[288,432]{1,0:T(8,128)(2,1)S(1)}, bf16[288,432]{1,0:T(8,128)(2,1)S(1)}, u32[]{:S(2)}, u32[]{:S(2)}) %collective-permute-start.46) | collective-permute-done | bytes 248864 | tf_op jit(solution)/shard_map/ppermute | solution.py:49
  (662 shorter events, 384.3 us)
Async XLA Ops:
  21.5 44.9 %collective-permute-start.3 = (bf16[288,720]{1,0:T(8,128)(2,1)S(1)}, bf16[288,720]{1,0:T(8,128)(2,1)S(1)}, u32[]{:S(2)}, u32[]{:S(2)}) collective-permute-start(bf16[288,720]{1,0:T(8,128)(2,1)S(1)} %concatenate.142), channel_id=1, source_target_pairs={{0,4},{1,5},{2,6},{3,7},{4,0},{5,1},{6,2},{7,3},{8,12},{9,13},{10,... | collective-permute-start | bytes 1244168 | tf_op jit(solution)/shard_map/ppermute | solution.py:49
  28.6 75.5 %all-to-all-start = ((bf16[8,144,430]{2,1,0:T(8,128)(2,1)}), bf16[8,144,430]{2,1,0:T(8,128)(2,1)S(1)}, u32[]{:S(2)}, u32[]{:S(2)}) async-start(bf16[8,144,430]{2,1,0:T(8,128)(2,1)} %pad_maximum_fusion.20), calls=%async_computation | async-start | bytes 2359296 | tf_op jit(solution)/shard_map/all_to_all | solution.py:324
  32.2 64.1 %collective-permute-start.9 = (bf16[288,432]{1,0:T(8,128)(2,1)}, bf16[288,432]{1,0:T(8,128)(2,1)}, u32[]{:S(2)}, u32[]{:S(2)}) collective-permute-start(bf16[288,432]{1,0:T(8,128)(2,1)} %pad_maximum_fusion.33), channel_id=1, source_target_pairs={{0,4},{1,5},{2,6},{3,7},{4,0},{5,1},{6,2},{7,3},{8,12},{9,13},{10,... | collective-permute-start | bytes 746504 | tf_op jit(solution)/shard_map/ppermute | solution.py:49
  35.1 63.1 %collective-permute-start.8 = (bf16[288,432]{1,0:T(8,128)(2,1)}, bf16[288,432]{1,0:T(8,128)(2,1)}, u32[]{:S(2)}, u32[]{:S(2)}) collective-permute-start(bf16[288,432]{1,0:T(8,128)(2,1)} %pad_maximum_fusion.33), channel_id=1, source_target_pairs={{0,2},{1,3},{2,0},{3,1},{4,6},{5,7},{6,4},{7,5},{8,10},{9,11},{10,... | collective-permute-start | bytes 746504 | tf_op jit(solution)/shard_map/ppermute | solution.py:49
  36.6 51.0 %collective-permute-start.4 = (bf16[288,720]{1,0:T(8,128)(2,1)S(1)}, bf16[288,720]{1,0:T(8,128)(2,1)S(1)}, u32[]{:S(2)}, u32[]{:S(2)}) collective-permute-start(bf16[288,720]{1,0:T(8,128)(2,1)S(1)} %concatenate.142), channel_id=1, source_target_pairs={{0,6},{1,7},{2,4},{3,5},{4,2},{5,3},{6,0},{7,1},{8,14},{9,15},{10,... | collective-permute-start | bytes 1244168 | tf_op jit(solution)/shard_map/ppermute | solution.py:49
  36.6 49.8 %collective-permute-start.2 = (bf16[288,720]{1,0:T(8,128)(2,1)S(1)}, bf16[288,720]{1,0:T(8,128)(2,1)S(1)}, u32[]{:S(2)}, u32[]{:S(2)}) collective-permute-start(bf16[288,720]{1,0:T(8,128)(2,1)S(1)} %concatenate.142), channel_id=1, source_target_pairs={{0,2},{1,3},{2,0},{3,1},{4,6},{5,7},{6,4},{7,5},{8,10},{9,11},{10,... | collective-permute-start | bytes 1244168 | tf_op jit(solution)/shard_map/ppermute | solution.py:49
  92.8 59.4 %collective-permute-start.5 = (bf16[288,2880]{1,0:T(8,128)(2,1)S(1)}, bf16[288,2880]{1,0:T(8,128)(2,1)}, u32[]{:S(2)}, u32[]{:S(2)}) collective-permute-start(bf16[288,2880]{1,0:T(8,128)(2,1)S(1)} %concatenate.144), channel_id=1, source_target_pairs={{0,16},{8,24},{16,0},{24,8},{1,17},{9,25},{17,1},{25,9},{2,18},{10... | collective-permute-start | bytes 4976648 | tf_op jit(solution)/shard_map/ppermute | solution.py:45
  103.6 48.6 %collective-permute-start.10 = (bf16[288,1728]{1,0:T(8,128)(2,1)}, bf16[288,1728]{1,0:T(8,128)(2,1)}, u32[]{:S(2)}, u32[]{:S(2)}) collective-permute-start(bf16[288,1728]{1,0:T(8,128)(2,1)} %concatenate.146), channel_id=1, source_target_pairs={{0,16},{8,24},{16,0},{24,8},{1,17},{9,25},{17,1},{25,9},{2,18},{10... | collective-permute-start | bytes 2985992 | tf_op jit(solution)/shard_map/ppermute | solution.py:45
  105.6 47.1 %collective-permute-start = (bf16[1152,430]{0,1:T(8,128)(2,1)}, bf16[1152,430]{0,1:T(8,128)(2,1)}, u32[]{:S(2)}, u32[]{:S(2)}) collective-permute-start(bf16[1152,430]{0,1:T(8,128)(2,1)} %copy.207), channel_id=1, source_target_pairs={{0,0},{1,1},{2,8},{3,9},{4,4},{5,5},{6,12},{7,13},{8,2},{9,3},{10,... | collective-permute-start | bytes 2972168 | tf_op jit(solution)/shard_map/ppermute | solution.py:192
  115.1 50.9 %collective-permute-start.11 = (bf16[288,1728]{1,0:T(8,128)(2,1)}, bf16[288,1728]{1,0:T(8,128)(2,1)}, u32[]{:S(2)}, u32[]{:S(2)}) collective-permute-start(bf16[288,1728]{1,0:T(8,128)(2,1)} %concatenate.146), channel_id=1, source_target_pairs={{0,8},{8,0},{16,24},{24,16},{1,9},{9,1},{17,25},{25,17},{2,10},{10... | collective-permute-start | bytes 2985992 | tf_op jit(solution)/shard_map/ppermute | solution.py:45
  123.9 60.2 %collective-permute-start.6 = (bf16[288,2880]{1,0:T(8,128)(2,1)S(1)}, bf16[288,2880]{1,0:T(8,128)(2,1)}, u32[]{:S(2)}, u32[]{:S(2)}) collective-permute-start(bf16[288,2880]{1,0:T(8,128)(2,1)S(1)} %concatenate.144), channel_id=1, source_target_pairs={{0,8},{8,0},{16,24},{24,16},{1,9},{9,1},{17,25},{25,17},{2,10},{10... | collective-permute-start | bytes 4976648 | tf_op jit(solution)/shard_map/ppermute | solution.py:45
  202.3 36.1 %collective-permute-start.26 = (bf16[288,576]{1,0:T(8,128)(2,1)}, bf16[288,576]{1,0:T(8,128)(2,1)}, u32[]{:S(2)}, u32[]{:S(2)}) collective-permute-start(bf16[288,576]{1,0:T(8,128)(2,1)} %param.45), channel_id=1, source_target_pairs={{0,4},{1,5},{2,6},{3,7},{4,0},{5,1},{6,2},{7,3},{8,12},{9,13},{10,... | collective-permute-start | bytes 995336 | tf_op jit(solution)/shard_map/ppermute | solution.py:49
  222.6 35.5 %collective-permute-start.16 = (bf16[1152,256]{1,0:T(8,128)(2,1)}, bf16[1152,256]{1,0:T(8,128)(2,1)}, u32[]{:S(2)}, u32[]{:S(2)}) collective-permute-start(bf16[1152,256]{1,0:T(8,128)(2,1)} %fusion.73), channel_id=1, source_target_pairs={{0,1},{1,0},{2,3},{3,2},{4,5},{5,4},{6,7},{7,6},{8,9},{9,8},{10,11... | collective-permute-start | bytes 1769480 | tf_op jit(solution)/shard_map/ppermute | solution.py:49
  223.9 59.4 %all-to-all-start.2 = ((bf16[8,144,256]{2,1,0:T(8,128)(2,1)}), bf16[8,144,256]{2,1,0:T(8,128)(2,1)}, u32[]{:S(2)}, u32[]{:S(2)}) async-start(bf16[8,144,256]{2,1,0:T(8,128)(2,1)} %bitcast.194), calls=%async_computation.2 | async-start | bytes 1179648 | tf_op jit(solution)/shard_map/all_to_all | solution.py:212
  250.7 66.0 %collective-permute-start.27 = (bf16[288,2304]{1,0:T(8,128)(2,1)}, bf16[288,2304]{1,0:T(8,128)(2,1)}, u32[]{:S(2)}, u32[]{:S(2)}) collective-permute-start(bf16[288,2304]{1,0:T(8,128)(2,1)} %concatenate.155), channel_id=1, source_target_pairs={{0,16},{8,24},{16,0},{24,8},{1,17},{9,25},{17,1},{25,9},{2,18},{10... | collective-permute-start | bytes 3981320 | tf_op jit(solution)/shard_map/ppermute | solution.py:45
  269.0 48.3 %collective-permute-start.17 = (bf16[1152,256]{1,0:T(8,128)(2,1)}, bf16[1152,256]{1,0:T(8,128)(2,1)}, u32[]{:S(2)}, u32[]{:S(2)}) collective-permute-start(bf16[1152,256]{1,0:T(8,128)(2,1)} %slice.1212), channel_id=1, source_target_pairs={{0,1},{1,0},{2,3},{3,2},{4,5},{5,4},{6,7},{7,6},{8,9},{9,8},{10,11... | collective-permute-start | bytes 1769480 | tf_op jit(solution)/shard_map/ppermute | solution.py:49
  283.3 66.5 %collective-permute-start.28 = (bf16[288,2304]{1,0:T(8,128)(2,1)}, bf16[288,2304]{1,0:T(8,128)(2,1)}, u32[]{:S(2)}, u32[]{:S(2)}) collective-permute-start(bf16[288,2304]{1,0:T(8,128)(2,1)} %concatenate.155), channel_id=1, source_target_pairs={{0,8},{8,0},{16,24},{24,16},{1,9},{9,1},{17,25},{25,17},{2,10},{10... | collective-permute-start | bytes 3981320 | tf_op jit(solution)/shard_map/ppermute | solution.py:45
  316.7 41.4 %collective-permute-start.23 = (bf16[288,2304]{1,0:T(8,128)(2,1)}, bf16[288,2304]{1,0:T(8,128)(2,1)}, u32[]{:S(2)}, u32[]{:S(2)}) collective-permute-start(bf16[288,2304]{1,0:T(8,128)(2,1)} %concatenate.153), channel_id=1, source_target_pairs={{0,8},{8,0},{16,24},{24,16},{1,9},{9,1},{17,25},{25,17},{2,10},{10... | collective-permute-start | bytes 3981320 | tf_op jit(solution)/shard_map/ppermute | solution.py:45
  397.8 169.9 %collective-permute-start.73 = (bf16[576,2304]{1,0:T(8,128)(2,1)}, bf16[576,2304]{1,0:T(8,128)(2,1)}, u32[]{:S(2)}, u32[]{:S(2)}) collective-permute-start(bf16[576,2304]{1,0:T(8,128)(2,1)} %convolution_convert_fusion), channel_id=1, source_target_pairs={{0,8},{8,0},{16,24},{24,16},{1,9},{9,1},{17,25},{25,17},{2,10},{10... | collective-permute-start | bytes 7962632 | tf_op jit(solution)/shard_map/ppermute | solution.py:45
  430.4 140.6 %collective-permute-start.68 = (bf16[576,2304]{1,0:T(8,128)(2,1)}, bf16[576,2304]{1,0:T(8,128)(2,1)}, u32[]{:S(2)}, u32[]{:S(2)}) collective-permute-start(bf16[576,2304]{1,0:T(8,128)(2,1)} %convolution_convert_fusion.1), channel_id=1, source_target_pairs={{0,8},{8,0},{16,24},{24,16},{1,9},{9,1},{17,25},{25,17},{2,10},{10... | collective-permute-start | bytes 7962632 | tf_op jit(solution)/shard_map/ppermute | solution.py:45
  435.9 56.9 %collective-permute-start.32 = (bf16[1152,256]{1,0:T(8,128)(2,1)}, bf16[1152,256]{1,0:T(8,128)(2,1)}, u32[]{:S(2)}, u32[]{:S(2)}) collective-permute-start(bf16[1152,256]{1,0:T(8,128)(2,1)} %pad_maximum_fusion.29), channel_id=1, source_target_pairs={{0,0},{1,1},{2,8},{3,9},{4,4},{5,5},{6,12},{7,13},{8,2},{9,3},{10,... | collective-permute-start | bytes 1769480 | tf_op jit(solution)/shard_map/ppermute | solution.py:192
  487.0 56.3 %collective-permute-start.38 = (bf16[1152,256]{1,0:T(8,128)(2,1)S(1)}, bf16[1152,256]{1,0:T(8,128)(2,1)}, u32[]{:S(2)}, u32[]{:S(2)}) collective-permute-start(bf16[1152,256]{1,0:T(8,128)(2,1)S(1)} %multiply_convert_fusion.1), channel_id=1, source_target_pairs={{0,1},{1,0},{2,3},{3,2},{4,5},{5,4},{6,7},{7,6},{8,9},{9,8},{10,11... | collective-permute-start | bytes 1769480 | tf_op jit(solution)/shard_map/ppermute | solution.py:49
  564.6 60.1 %collective-permute-start.39 = (bf16[1152,512]{1,0:T(8,128)(2,1)}, bf16[1152,512]{1,0:T(8,128)(2,1)}, u32[]{:S(2)}, u32[]{:S(2)}) collective-permute-start(bf16[1152,512]{1,0:T(8,128)(2,1)} %slice.834), channel_id=1, source_target_pairs={{0,8},{8,0},{16,24},{24,16},{1,9},{9,1},{17,25},{25,17},{2,10},{10... | collective-permute-start | bytes 3538952 | tf_op jit(solution)/shard_map/ppermute | solution.py:45
  601.9 37.4 %collective-permute-start.74 = (bf16[288,2304]{1,0:T(8,128)(2,1)}, bf16[288,2304]{1,0:T(8,128)(2,1)}, u32[]{:S(2)}, u32[]{:S(2)}) collective-permute-start(bf16[288,2304]{1,0:T(8,128)(2,1)} %fusion.10), channel_id=1, source_target_pairs={{0,16},{8,24},{16,0},{24,8},{1,17},{9,25},{17,1},{25,9},{2,18},{10... | collective-permute-start | bytes 3981320 | tf_op jit(solution)/shard_map/ppermute | solution.py:45
  613.1 48.4 %collective-permute-start.69 = (bf16[288,2304]{1,0:T(8,128)(2,1)}, bf16[288,2304]{1,0:T(8,128)(2,1)}, u32[]{:S(2)}, u32[]{:S(2)}) collective-permute-start(bf16[288,2304]{1,0:T(8,128)(2,1)} %fusion.9), channel_id=1, source_target_pairs={{0,16},{8,24},{16,0},{24,8},{1,17},{9,25},{17,1},{25,9},{2,18},{10... | collective-permute-start | bytes 3981320 | tf_op jit(solution)/shard_map/ppermute | solution.py:45
  639.0 61.7 %collective-permute-start.43 = (bf16[576,1728]{1,0:T(8,128)(2,1)}, bf16[576,1728]{1,0:T(8,128)(2,1)}, u32[]{:S(2)}, u32[]{:S(2)}) collective-permute-start(bf16[576,1728]{1,0:T(8,128)(2,1)} %convolution_convert_fusion.2), channel_id=1, source_target_pairs={{0,8},{8,0},{16,24},{24,16},{1,9},{9,1},{17,25},{25,17},{2,10},{10... | collective-permute-start | bytes 5971976 | tf_op jit(solution)/shard_map/ppermute | solution.py:45
  645.8 61.9 %collective-permute-start.75 = (bf16[288,576]{1,0:T(8,128)(2,1)}, bf16[288,576]{1,0:T(8,128)(2,1)}, u32[]{:S(2)}, u32[]{:S(2)}) collective-permute-start(bf16[288,576]{1,0:T(8,128)(2,1)} %get-tuple-element.248), channel_id=1, source_target_pairs={{0,2},{1,3},{2,0},{3,1},{4,6},{5,7},{6,4},{7,5},{8,10},{9,11},{10,... | collective-permute-start | bytes 995336 | tf_op jit(solution)/shard_map/ppermute | solution.py:49
  645.8 61.9 %collective-permute-start.77 = (bf16[288,576]{1,0:T(8,128)(2,1)}, bf16[288,576]{1,0:T(8,128)(2,1)}, u32[]{:S(2)}, u32[]{:S(2)}) collective-permute-start(bf16[288,576]{1,0:T(8,128)(2,1)} %get-tuple-element.249), channel_id=1, source_target_pairs={{0,6},{1,7},{2,4},{3,5},{4,2},{5,3},{6,0},{7,1},{8,14},{9,15},{10,... | collective-permute-start | bytes 995336 | tf_op jit(solution)/shard_map/ppermute | solution.py:49
  661.6 49.4 %collective-permute-start.76 = (bf16[288,576]{1,0:T(8,128)(2,1)}, bf16[288,576]{1,0:T(8,128)(2,1)}, u32[]{:S(2)}, u32[]{:S(2)}) collective-permute-start(bf16[288,576]{1,0:T(8,128)(2,1)} %get-tuple-element.250), channel_id=1, source_target_pairs={{0,4},{1,5},{2,6},{3,7},{4,0},{5,1},{6,2},{7,3},{8,12},{9,13},{10,... | collective-permute-start | bytes 995336 | tf_op jit(solution)/shard_map/ppermute | solution.py:49
  696.9 54.1 %all-to-all-start.3 = ((bf16[8,144,256]{2,1,0:T(8,128)(2,1)}), bf16[8,144,256]{2,1,0:T(8,128)(2,1)S(1)}, u32[]{:S(2)}, u32[]{:S(2)}) async-start(bf16[8,144,256]{2,1,0:T(8,128)(2,1)} %bitcast.46), calls=%async_computation.3 | async-start | bytes 1179648 | tf_op jit(solution)/shard_map/all_to_all | solution.py:217
  707.6 41.1 %collective-permute-start.71 = (bf16[288,576]{1,0:T(8,128)(2,1)}, bf16[288,576]{1,0:T(8,128)(2,1)S(1)}, u32[]{:S(2)}, u32[]{:S(2)}) collective-permute-start(bf16[288,576]{1,0:T(8,128)(2,1)} %get-tuple-element.253), channel_id=1, source_target_pairs={{0,4},{1,5},{2,6},{3,7},{4,0},{5,1},{6,2},{7,3},{8,12},{9,13},{10,... | collective-permute-start | bytes 995336 | tf_op jit(solution)/shard_map/ppermute | solution.py:49
  707.7 44.7 %collective-permute-start.44 = (bf16[288,1728]{1,0:T(8,128)(2,1)}, bf16[288,1728]{1,0:T(8,128)(2,1)}, u32[]{:S(2)}, u32[]{:S(2)}) collective-permute-start(bf16[288,1728]{1,0:T(8,128)(2,1)} %fusion.12), channel_id=1, source_target_pairs={{0,16},{8,24},{16,0},{24,8},{1,17},{9,25},{17,1},{25,9},{2,18},{10... | collective-permute-start | bytes 2985992 | tf_op jit(solution)/shard_map/ppermute | solution.py:45
  (182 other events, 2057.0 us)
